TPU v7x, 128 devices: a whole 4x4x4 slice. The times are simulated.
128 devices in a mesh: dp: 32 (over y, z, core), section: 4 (over x).
Axes of the slice: x: 4, y: 4, z: 4, core: 2. Of those that a mesh axis runs over, the one named last changes fastest.
Arguments:
- hidden_in: bfloat16 [2, 2048, 8192], P(None, 'dp'), may hold values from -6 to 6
- out_grad: bfloat16 [2, 2048, 8192], P(None, 'dp'), may hold values from -0.4375 to 0.4375
- gains: float32 [2, 4, 4096], P(None, 'section'), may hold values from 0.1 to 1.9
- blocks: bfloat16 [2, 4, 256, 128, 128], P(None, 'section'), may hold values from -0.1875 to 0.1875
- block_rows: int32 [2, 4, 256], P(None, 'section'), may hold values from 0 to 31, as said below
- block_cols: int32 [2, 4, 256], P(None, 'section'), may hold values from 0 to 31, as said below
- block_counts: int32 [2, 4], P(None, 'section'), may hold values from 64 to 256, as said below
Outputs:
- block_grads: bfloat16 [2, 4, 256, 128, 128], P(None, 'section', 'dp')
Inputs may be any that keep to these rules, and one draw needn't show every extreme that they name: Slot n of layer (t, s) is the tile at block row block_rows[t, s, n]; the 256 slots of one layer name different tiles. `block_cols`: block column of each slot, paired with block_rows. `block_counts`: only slots below a layer's count hold weights; the others are padding. Counts differ between layers; in every draw one layer has 256 live slots and another a quarter of 256.
All inputs are finite; a program needn't handle non-finite values.
Results may differ from a plain program's by a relative error of at most 0.023.
Values may be sent and summed in bfloat16 or wider, within the bound.
No kernel may reach another device: no remote copies, remote signals or barrier semaphores. Data moves between devices by JAX's collectives and lax.ppermute only.
A program may use at most 320 MiB of HBM per device.

v0:
```python
import jax
import jax.numpy as jnp
from jax import lax
from jax.experimental import pallas as pl
from jax.experimental.pallas import tpu as pltpu
from jax.sharding import PartitionSpec as P

norm_eps = 1e-05
LAG = 1
UNROLL = 32
STEP = 8
FLIP = 8
f32 = jnp.float32
bf16 = jnp.bfloat16
VM = pl.BlockSpec(memory_space=pltpu.VMEM)
SM = pl.BlockSpec(memory_space=pltpu.SMEM)
HBM = pl.BlockSpec(memory_space=pltpu.HBM)
LIMIT = 10 * 2**20
GRAD_LIMIT = 12 * 2**20


def split_pair(value, width):
    high = value.astype(bf16).astype(f32)
    low = value - high
    lane = lax.broadcasted_iota(jnp.int32, (value.shape[0], width), 1)
    return jnp.where(lane == 0, high, jnp.where(lane == 1, low, 0.0)).astype(bf16)


def tile_loop(gather_from, scatter_to, first, live, trash, source, weights, offset, acc):
    def group(g, carry):
        for k in range(UNROLL):
            n = g * UNROLL + k
            put = jnp.where(n < live, scatter_to[first + n], trash)
            acc[put] += jnp.dot(source[gather_from[first + n]], weights[offset + n], preferred_element_type=f32)
        return carry

    lax.fori_loop(0, (live + UNROLL - 1) // UNROLL, group, 0)


def each_block(count, visit, carry=0):
    def step(i, carry):
        for k in range(STEP):
            carry = visit(i * STEP + k, carry)
        return carry

    return lax.fori_loop(0, count // STEP, step, carry)


class Plan:
    def __init__(self, sections, turns, slots, tile, grid, tokens):
        self.sections, self.turns, self.slots = sections, turns, slots
        self.tile, self.grid = tile, grid
        self.units = sections * LAG
        self.rows = tokens // self.units
        self.span = (sections - 1) * LAG
        self.bundle = 2 * LAG
        self.ticks = turns * self.units + self.span
        self.section, self.half = turns, turns + 1

    def piece(self, dtype, extra=0):
        return jax.ShapeDtypeStruct((self.grid + extra, self.rows, self.tile), dtype)


def lane_sum(value):
    return jnp.sum(value.astype(f32), axis=-1, keepdims=True)


def tick_call(plan, tick, order, forward, named, stores, pack, turned, last):
    G, T, B, M = plan.grid, plan.rows, plan.tile, plan.units
    width = 2 * G * B
    named = {name: value for name, value in named.items() if value is not None}
    names = list(named)
    use_entering, use_prev = "entering" in named, "prev" in named
    first_turn = 0 if forward else 1
    turns_here = [first_turn] * use_entering + [1 - first_turn] * use_prev
    critical, early = "critical" in named, "early" in named
    early_at = (order - plan.span) % plan.bundle
    saves = ["kept", "slope", "scale"] if forward else ["grad"]
    piece = tick if tick < plan.span else tick - plan.turns * M
    turning = forward and (tick < plan.span or tick >= plan.turns * M)
    share = FLIP * -(-plan.slots // (plan.span * FLIP))
    piece_size = min(share, plan.slots - share * piece) if turning else 0

    shapes = {"sent": (VM, plan.piece(bf16, 1))}
    for name in saves:
        shape, kind = ((T, B), f32) if name == "scale" else ((G, T, B), bf16)
        shapes[name + "_out"] = (HBM, jax.ShapeDtypeStruct(shape, kind) if last else pltpu.HBM(shape, kind))
    alias_from = {}
    for turn in turns_here:
        shapes["store%d" % turn] = (HBM, pltpu.HBM((M, G, T, B), bf16))
        if stores[turn] is not None:
            alias_from["store%d" % turn] = stores[turn]
    if turning:
        for turn in range(2):
            shapes["turned%d" % turn] = (HBM, pltpu.HBM((plan.slots, B, B), bf16))
            if turned[turn] is not None:
                alias_from["turned%d" % turn] = turned[turn]
    if pack:
        shapes["bundle"] = (VM, jax.ShapeDtypeStruct((plan.bundle, G, T, B), bf16))
    out_names = list(shapes)
    scratch = {"source": pltpu.VMEM((G, T, B), bf16), "acc": pltpu.VMEM((G + 1, T, B), f32)}
    for name in saves:
        scratch[name + "_new"] = pltpu.VMEM((T, B), f32) if name == "scale" else pltpu.VMEM((G, T, B), bf16)
    if turning:
        scratch["flipped"] = pltpu.VMEM((2, piece_size, B, B), bf16)
    if forward and tick < M:
        scratch["extra"] = pltpu.VMEM((T, B), f32)
    scratch["sems"] = pltpu.SemaphoreType.DMA((5,))
    if pack:
        scratch["pack_sems"] = pltpu.SemaphoreType.DMA((plan.bundle,))

    def kernel(*refs):
        ref = dict(zip(names, refs))
        rest = refs[len(names) + len(pack) + len(alias_from):]
        older_sent = refs[len(names):len(names) + len(pack)]
        out = dict(zip(out_names, rest))
        own = dict(zip(scratch, rest[len(out_names):]))
        tab, sent, acc, source, sems = ref["info"], out["sent"], own["acc"], own["source"], own["sems"]
        step = tick - LAG * tab[plan.section]
        active = (step >= 0) & (step < 2 * M)
        parity = tab[plan.section] % 2
        entry = (parity if forward else 1 - parity) * (G * B)
        packing = [pltpu.make_async_copy(old.at[pl.ds(0, G)], out["bundle"].at[i], own["pack_sems"].at[i]) for i, old in enumerate(pack and older_sent)]
        for copy in packing:
            copy.start()

        def arriving(turn, unit, b):
            if use_entering:
                value = ref["entering"][unit, :, pl.ds(pl.multiple_of(entry + b * B, B), B)].astype(f32)
            if use_prev:
                older = ref["prev"][b].astype(f32)
                value = jnp.where(turn == first_turn, value, older) if use_entering else older
            if early:
                value = value + ref["early"][early_at, b].astype(f32)
            if critical:
                value = value + ref["critical"][b].astype(f32)
            return value.astype(bf16)

        def send(b, value):
            sent[b] = value
            if pack:
                out["bundle"][plan.bundle - 1, b] = value

        def keep(turn, unit, copies):
            for place in turns_here:
                @pl.when(turn == place)
                def _():
                    pltpu.make_async_copy(source, out["store%d" % place].at[unit], sems.at[0]).start()
            for copy in copies:
                copy.start()
            acc[...] = jnp.zeros_like(acc)

        def multiply(turn):
            live = tab[turn]
            gather_from, scatter_to = (ref["rows"], ref["cols"]) if forward else (ref["cols"], ref["rows"])
            if forward:
                tile_loop(gather_from, scatter_to, turn * plan.slots, live, G, source, ref["weights"], turn * plan.slots, acc)
            for place in turns_here * (not forward):
                @pl.when(turn == place)
                def _():
                    tile_loop(gather_from, scatter_to, place * plan.slots, live, G, source, ref["weights%d" % place], 0, acc)

        @pl.when(active)
        def _():
            turn = jnp.where(step >= M, 1, 0)
            unit = step - turn * M

            def gain(b):
                return ref["gains"][turn * G + b]

            if forward:
                kept, slope, scale = own["kept_new"], own["slope_new"], own["scale_new"]

                def enter(b, squares):
                    value = arriving(turn, unit, b)
                    kept[b] = value
                    value = value.astype(f32)
                    return squares + value * value

                square = lane_sum(each_block(G, enter, jnp.zeros((T, B), f32)))
                total = square
                if critical:
                    total = total + lane_sum(ref["critical"][G])
                if tick < M:
                    extra = own["extra"]
                    extra[...] = jnp.zeros_like(extra)

                    @pl.when(tab[plan.section] == 0)
                    def _():
                        def other(b, squares):
                            value = ref["entering"][unit, :, pl.ds(pl.multiple_of((G + b) * B, B), B)].astype(f32)
                            return squares + value * value

                        extra[...] = each_block(G, other, jnp.zeros((T, B), f32))

                    total = total + lane_sum(extra[...])
                inv_rms = lax.rsqrt(total / width + norm_eps)
                scale[...] = jnp.broadcast_to(inv_rms, (T, B))

                def normalize(b, carry):
                    source[b] = (kept[b].astype(f32) * inv_rms * gain(b)).astype(bf16)
                    return carry

                each_block(G, normalize)
                copies = [pltpu.make_async_copy(kept, out["kept_out"], sems.at[1]),
                          pltpu.make_async_copy(scale, out["scale_out"], sems.at[2])]
                keep(turn, unit, copies)
                multiply(turn)

                def activate(b, carry):
                    mixed = acc[b]
                    gate = jax.nn.sigmoid(mixed)
                    send(b, (mixed * gate).astype(bf16))
                    slope[b] = (gate * (1.0 + mixed * (1.0 - gate))).astype(bf16)
                    return carry

                half = G // 2
                for part in range(2):
                    each_block(half, lambda b, carry: activate(part * half + b, carry))
                    where = pl.ds(part * half, half)
                    copies.append(pltpu.make_async_copy(slope.at[where], out["slope_out"].at[where], sems.at[3 + part]))
                    copies[-1].start()
                sent[G] = split_pair(square, B)
            else:
                grad = own["grad_new"]

                def enter(b, carry):
                    value = arriving(turn, unit, b)
                    grad[b] = value
                    source[b] = (value.astype(f32) * ref["slope"][b].astype(f32)).astype(bf16)
                    return carry

                each_block(G, enter)
                copies = [pltpu.make_async_copy(grad, out["grad_out"], sems.at[1])]
                keep(turn, unit, copies)
                multiply(turn)

                def weigh(b, inner):
                    weighted = acc[b] * gain(b)
                    acc[b] = weighted
                    return inner + weighted * ref["kept"][b].astype(f32)

                inner = lane_sum(each_block(G, weigh, jnp.zeros((T, B), f32)))
                inv_rms = ref["scale"][:, 0:1]
                factor = inv_rms * inv_rms * inv_rms / width * inner
                total = factor
                if critical:
                    total = total + lane_sum(ref["critical"][G])

                def leave(b, carry):
                    send(b, (inv_rms * acc[b] - total * ref["kept"][b].astype(f32)).astype(bf16))
                    return carry

                each_block(G, leave)
                sent[G] = split_pair(factor, B)
            pltpu.make_async_copy(source, out["store%d" % turns_here[0]].at[unit], sems.at[0]).wait()
            for copy in copies:
                copy.wait()

        @pl.when(jnp.logical_not(active))
        def _():
            sent[...] = jnp.zeros_like(sent)
            if pack:
                out["bundle"][plan.bundle - 1] = jnp.zeros((G, T, B), bf16)
            if turning:
                flipped = own["flipped"]
                moves = []
                for place in range(2):

                    def flip(i, carry):
                        for k in range(FLIP):
                            at = i * FLIP + k
                            flipped[place, at] = ref["weights"][place * plan.slots + piece * share + at].T
                        return carry

                    lax.fori_loop(0, piece_size // FLIP, flip, 0)
                    moves.append(pltpu.make_async_copy(
                        flipped.at[place], out["turned%d" % place].at[pl.ds(piece * share, piece_size)], sems.at[place]))
                    moves[-1].start()
                for copy in moves:
                    copy.wait()

        for copy in packing:
            copy.wait()

    ins = list(named.values()) + list(pack) + list(alias_from.values())
    outs = pl.pallas_call(
        kernel,
        in_specs=[SM] * 3 + [VM] * (len(names) - 3 + len(pack)) + [HBM] * len(alias_from),
        out_specs=[spec for spec, _ in shapes.values()],
        out_shape=[shape for _, shape in shapes.values()],
        input_output_aliases={len(names) + len(pack) + i: out_names.index(name) for i, name in enumerate(alias_from)},
        scratch_shapes=list(scratch.values()),
        compiler_params=pltpu.CompilerParams(vmem_limit_bytes=LIMIT),
        name="forward_tick" if forward else "backward_tick",
    )(*ins)
    return dict(zip(out_names, outs))


def tile_grads(plan, turn, info, rows, cols, normed_pair, error_pair, share, parts):
    G, T, B, M = plan.grid, plan.rows, plan.tile, plan.units
    local = plan.slots // parts
    steps = 8
    chunk = local // steps
    tokens = M * T

    def kernel(tab, rows_at, cols_at, *refs):
        normeds, errors = refs[:parts], refs[parts:2 * parts]
        out, turned, flat = refs[2 * parts:]
        step = pl.program_id(0)

        @pl.when(step == 0)
        def _():
            for b in range(G):
                for p in range(parts):
                    for m in range(M):
                        at = p * tokens + m * T
                        flat[b, at:at + T, :] = errors[p][m, b]
                    whole = jnp.concatenate([normeds[p][m, b] for m in range(M)], axis=0)
                    turned[b, :, p * tokens:(p + 1) * tokens] = whole.T

        half = tab[plan.half]
        live = tab[turn]
        for k in range(chunk):
            i = step * chunk + k
            n = (i // share) * (share * parts) + half * share + i % share
            at = turn * plan.slots + n
            made = jnp.dot(turned[rows_at[at]], flat[cols_at[at]], preferred_element_type=f32)
            out[k] = jnp.where(n < live, made, 0.0).astype(bf16)

    whole = pl.BlockSpec((M, G, T, B), lambda i, *_: (0, 0, 0, 0))
    return pl.pallas_call(
        kernel,
        grid_spec=pltpu.PrefetchScalarGridSpec(
            num_scalar_prefetch=3,
            grid=(steps,),
            in_specs=[whole] * (2 * parts),
            out_specs=pl.BlockSpec((chunk, B, B), lambda i, *_: (i, 0, 0)),
            scratch_shapes=[pltpu.VMEM((G, B, parts * tokens), bf16), pltpu.VMEM((G, parts * tokens, B), bf16)],
        ),
        out_shape=pltpu.HBM((local, B, B), bf16),
        compiler_params=pltpu.CompilerParams(vmem_limit_bytes=GRAD_LIMIT),
        cost_estimate=pl.CostEstimate(flops=2 * local * B * B * parts * tokens, transcendentals=0, bytes_accessed=24 * 2**20),
        name="tile_grads",
    )(info, rows, cols, *normed_pair, *error_pair)


def sum_parts(parts):
    def kernel(given, out):
        total = given[0].astype(f32)
        for i in range(1, parts.shape[0]):
            total = total + given[i].astype(f32)
        out[...] = total.astype(bf16)

    rest = parts.shape[2:]
    return pl.pallas_call(
        kernel,
        grid=(parts.shape[1] // 2,),
        in_specs=[pl.BlockSpec((parts.shape[0], 2, *rest), lambda i: (0, i, 0, 0))],
        out_specs=pl.BlockSpec((2, *rest), lambda i: (i, 0, 0)),
        out_shape=jax.ShapeDtypeStruct(parts.shape[1:], bf16),
        compiler_params=pltpu.CompilerParams(vmem_limit_bytes=GRAD_LIMIT),
        name="sum_parts",
    )(parts)


def body(hidden_in, out_grad, gains, blocks, block_rows, block_cols, block_counts):
    sections = lax.axis_size("section")
    replicas = lax.axis_size("dp")
    section_pos = lax.axis_index("section").astype(jnp.int32)
    core = (lax.axis_index("dp") % 2).astype(jnp.int32)
    turns, slots, tile = blocks.shape[0], blocks.shape[2], blocks.shape[3]
    tokens = hidden_in.shape[0] * hidden_in.shape[1]
    half_width = hidden_in.shape[2] // 2
    grid = half_width // tile
    plan = Plan(sections, turns, slots, tile, grid, tokens)
    M, T = plan.units, plan.rows

    rows, cols = block_rows.reshape(-1), block_cols.reshape(-1)
    info = jnp.concatenate([block_counts.reshape(-1), section_pos[None], core[None]])
    entering = hidden_in.reshape(M, T, 2 * half_width)
    entering_grad = out_grad.reshape(M, T, 2 * half_width)
    weights = blocks.reshape(turns * slots, tile, tile)
    gain_rows = gains.reshape(turns * grid, 1, tile)

    def ring(part, by):
        return lax.ppermute(part, "section", [(i, (i + by) % sections) for i in range(sections)])

    def run(forward, weights, saved, hook):
        stores, turned = [None, None], [None, None]
        sents, ahead, bundles, kept = [], [], {}, []
        toward = 1 if forward else -1
        for order in range(plan.ticks):
            tick = order if forward else plan.ticks - 1 - order
            use_entering, use_prev = order < M + plan.span, order >= M
            named = dict(info=info, rows=rows, cols=cols, gains=gain_rows)
            if forward:
                named["weights"] = weights
            else:
                named["weights1"] = weights[1] if use_entering else None
                named["weights0"] = weights[0] if use_prev else None
            named["entering"] = (entering if forward else entering_grad) if use_entering else None
            if forward:
                named["prev"] = kept[order - M]["kept_out"] if use_prev else None
            else:
                named["kept"], named["slope"], named["scale"] = [saved[tick][name + "_out"] for name in ("kept", "slope", "scale")]
                named["prev"] = kept[order - M]["grad_out"] if use_prev else None
            named["critical"] = ahead[order - LAG] if order >= LAG else None
            named["early"] = bundles[(order - plan.span) // plan.bundle] if order >= plan.span else None
            pack = ()
            if order % plan.bundle == plan.bundle - 1 and order - plan.bundle + 1 + plan.span < plan.ticks:
                pack = tuple(sents[order - plan.bundle + 1:order])
            made = tick_call(plan, tick, order, forward, named, stores, pack, turned, order == plan.ticks - 1)
            sents.append(made["sent"])
            kept.append(made)
            stores = [made.get("store%d" % turn, stores[turn]) for turn in range(2)]
            turned = [made.get("turned%d" % turn, turned[turn]) for turn in range(2)]
            ahead.append(ring(made["sent"], toward) if order + LAG < plan.ticks else None)
            if pack:
                bundles[order // plan.bundle] = ring(made["bundle"], -toward)
            hook(order, ahead, stores)
        return kept, stores, turned

    saved, normed, turned = run(True, weights, None, lambda order, ahead, stores: None)

    chips = replicas // 2
    swap = [(i, i ^ 1) for i in range(replicas)]
    share = slots // replicas
    same_core = [[i for i in range(replicas) if i % 2 == c] for c in range(2)]

    def make_grads(turn, error):
        pairs = [[own, lax.ppermute(own, "dp", swap)] for own in (normed[turn], error)]
        return tile_grads(plan, turn, info, rows, cols, pairs[0], pairs[1], share, 2)

    def trade(part):
        return lax.all_to_all(
            part.reshape(chips, share, tile, tile), "dp", 0, 0, axis_index_groups=same_core, tiled=True
        )

    later = []

    def halfway(order, ahead, stores):
        if order == M + plan.span - 1:
            part, ahead[order] = lax.optimization_barrier((make_grads(1, stores[1]), ahead[order]))
            later.append(trade(part))

    _, errors, _ = run(False, turned, saved, halfway)
    sooner = trade(make_grads(0, errors[0]))
    results = [sum_parts(sooner), sum_parts(later[0])]
    return jnp.stack(results)[:, None]


def solution(mesh):
    return jax.shard_map(
        body,
        mesh=mesh,
        in_specs=(
            P(None, "dp", None),
            P(None, "dp", None),
            P(None, "section", None),
            P(None, "section", None, None, None),
            P(None, "section", None),
            P(None, "section", None),
            P(None, "section"),
        ),
        out_specs=P(None, "section", "dp", None, None),
        check_vma=False,
    )
```

profile of v0, /device:TPU:0, one launch (start us, length us, event | category | flops | bytes accessed | tf_op | source)
XLA Modules:
  0.0 373.0 jit_solution(10017040264369705488)
XLA Ops:
  0.7 5.8 %copy-done = bf16[2,1,256,128,128]{4,3,2,1,0:T(8,128)(2,1)S(1)} copy-done((bf16[2,1,256,128,128]{4,3,2,1,0:T(8,128)(2,1)S(1)}, bf16[2,1,256,128,128]{4,3,2,1,0:T(8,128)(2,1)}, u32[]{:S(2)}) %copy-start) | copy-done | bytes 16777240
  16.9 7.7 %collective-permute-done.refs_6_ = bf16[33,32,128]{2,1,0:T(8,128)(2,1)S(1)} collective-permute-done((bf16[33,32,128]{2,1,0:T(8,128)(2,1)S(1)}, bf16[33,32,128]{2,1,0:T(8,128)(2,1)S(1)}, u32[]{:S(2)}, u32[]{:S(2)}) %collective-permute-start) | collective-permute-done | bytes 270368 | tf_op jit(solution)/shard_map/ppermute | solution.py:387
  31.9 5.6 %collective-permute-done.1.refs_6_ = bf16[33,32,128]{2,1,0:T(8,128)(2,1)S(1)} collective-permute-done((bf16[33,32,128]{2,1,0:T(8,128)(2,1)S(1)}, bf16[33,32,128]{2,1,0:T(8,128)(2,1)S(1)}, u32[]{:S(2)}, u32[]{:S(2)}) %collective-permute-start.1) | collective-permute-done | bytes 270368 | tf_op jit(solution)/shard_map/ppermute | solution.py:387
  42.4 7.2 %collective-permute-done.2.refs_6_ = bf16[33,32,128]{2,1,0:T(8,128)(2,1)S(1)} collective-permute-done((bf16[33,32,128]{2,1,0:T(8,128)(2,1)S(1)}, bf16[33,32,128]{2,1,0:T(8,128)(2,1)S(1)}, u32[]{:S(2)}, u32[]{:S(2)}) %collective-permute-start.2) | collective-permute-done | bytes 270368 | tf_op jit(solution)/shard_map/ppermute | solution.py:387
  65.5 7.2 %collective-permute-done.5.refs_7_ = bf16[33,32,128]{2,1,0:T(8,128)(2,1)S(1)} collective-permute-done((bf16[33,32,128]{2,1,0:T(8,128)(2,1)S(1)}, bf16[33,32,128]{2,1,0:T(8,128)(2,1)S(1)}, u32[]{:S(2)}, u32[]{:S(2)}) %collective-permute-start.5) | collective-permute-done | bytes 270368 | tf_op jit(solution)/shard_map/ppermute | solution.py:387
  87.6 7.6 %collective-permute-done.9.refs_6_ = bf16[33,32,128]{2,1,0:T(8,128)(2,1)S(1)} collective-permute-done((bf16[33,32,128]{2,1,0:T(8,128)(2,1)S(1)}, bf16[33,32,128]{2,1,0:T(8,128)(2,1)S(1)}, u32[]{:S(2)}, u32[]{:S(2)}) %collective-permute-start.9) | collective-permute-done | bytes 270368 | tf_op jit(solution)/shard_map/ppermute | solution.py:387
  106.5 5.2 %forward_tick.19 = (bf16[33,32,128]{2,1,0:T(8,128)(2,1)S(1)}, bf16[32,32,128]{2,1,0:T(8,128)(2,1)}, bf16[32,32,128]{2,1,0:T(8,128)(2,1)}, f32[32,128]{1,0:T(8,12...) custom-call(s32[4]{0:T(128)S(1)} %pad_add_fusion.refs_0_.tab, ...), custom_call_target="tpu_custom_call", output_to_operand_aliasing={{4}: (8, {}), {5}: (9, {}), {6}: (10, {})} | custom-call | tf_op jit(solution)/shard_map/forward_tick/pallas_call | solution.py:287
  111.8 8.2 %collective-permute-done.12.refs_6_ = bf16[33,32,128]{2,1,0:T(8,128)(2,1)S(1)} collective-permute-done((bf16[33,32,128]{2,1,0:T(8,128)(2,1)S(1)}, bf16[33,32,128]{2,1,0:T(8,128)(2,1)S(1)}, u32[]{:S(2)}, u32[]{:S(2)}) %collective-permute-start.12) | collective-permute-done | bytes 270368 | tf_op jit(solution)/shard_map/ppermute | solution.py:387
  125.8 6.8 %collective-permute-done.14.refs_6_ = bf16[33,32,128]{2,1,0:T(8,128)(2,1)S(1)} collective-permute-done((bf16[33,32,128]{2,1,0:T(8,128)(2,1)S(1)}, bf16[33,32,128]{2,1,0:T(8,128)(2,1)S(1)}, u32[]{:S(2)}, u32[]{:S(2)}) %collective-permute-start.14) | collective-permute-done | bytes 270368 | tf_op jit(solution)/shard_map/ppermute | solution.py:387
  132.7 5.4 %forward_tick.21 = (bf16[33,32,128]{2,1,0:T(8,128)(2,1)}, bf16[32,32,128]{2,1,0:T(8,128)(2,1)S(1)}, bf16[32,32,128]{2,1,0:T(8,128)(2,1)S(1)}, f32[32,128]{1,0:T(...) custom-call(s32[4]{0:T(128)S(1)} %pad_add_fusion.refs_0_.tab, ...), custom_call_target="tpu_custom_call", output_to_operand_aliasing={{4}: (8, {}), {5}: (9, {}), {6}: (10, {})} | custom-call | tf_op jit(solution)/shard_map/forward_tick/pallas_call | solution.py:287
  146.3 6.5 %collective-permute-done.15.refs_9_ = bf16[33,32,128]{2,1,0:T(8,128)(2,1)S(1)} collective-permute-done((bf16[33,32,128]{2,1,0:T(8,128)(2,1)S(1)}, bf16[33,32,128]{2,1,0:T(8,128)(2,1)S(1)}, u32[]{:S(2)}, u32[]{:S(2)}) %collective-permute-start.15) | collective-permute-done | bytes 270368 | tf_op jit(solution)/shard_map/ppermute | solution.py:387
  153.6 7.6 %collective-permute-start.16 = (bf16[33,32,128]{2,1,0:T(8,128)(2,1)S(1)}, bf16[33,32,128]{2,1,0:T(8,128)(2,1)S(1)}, u32[]{:S(2)}, u32[]{:S(2)}) collective-permute-start(bf16[33,32,128]{2,1,0:T(8,128)(2,1)S(1)} %get-tuple-element.176), channel_id=1, source_target_pairs={{0,3},{1,0},{2,1},{3,2},{4,7},{5,4},{6,5},{7,6},{8,11},{9,8},{10,9... | collective-permute-start | bytes 811016 | tf_op jit(solution)/shard_map/ppermute | solution.py:387
  161.3 5.7 %collective-permute-done.16.refs_9_ = bf16[33,32,128]{2,1,0:T(8,128)(2,1)S(1)} collective-permute-done((bf16[33,32,128]{2,1,0:T(8,128)(2,1)S(1)}, bf16[33,32,128]{2,1,0:T(8,128)(2,1)S(1)}, u32[]{:S(2)}, u32[]{:S(2)}) %collective-permute-start.16) | collective-permute-done | bytes 270368 | tf_op jit(solution)/shard_map/ppermute | solution.py:387
  167.7 7.7 %collective-permute-start.17 = (bf16[33,32,128]{2,1,0:T(8,128)(2,1)S(1)}, bf16[33,32,128]{2,1,0:T(8,128)(2,1)S(1)}, u32[]{:S(2)}, u32[]{:S(2)}) collective-permute-start(bf16[33,32,128]{2,1,0:T(8,128)(2,1)S(1)} %get-tuple-element.188.refs_11_), channel_id=1, source_target_pairs={{0,3},{1,0},{2,1},{3,2},{4,7},{5,4},{6,5},{7,6},{8,11},{9,8},{10,9... | collective-permute-start | bytes 811016 | tf_op jit(solution)/shard_map/ppermute | solution.py:387
  183.4 5.3 %collective-permute-start.19 = (bf16[33,32,128]{2,1,0:T(8,128)(2,1)S(1)}, bf16[33,32,128]{2,1,0:T(8,128)(2,1)S(1)}, u32[]{:S(2)}, u32[]{:S(2)}) collective-permute-start(bf16[33,32,128]{2,1,0:T(8,128)(2,1)S(1)} %get-tuple-element.191), channel_id=1, source_target_pairs={{0,3},{1,0},{2,1},{3,2},{4,7},{5,4},{6,5},{7,6},{8,11},{9,8},{10,9... | collective-permute-start | bytes 811016 | tf_op jit(solution)/shard_map/ppermute | solution.py:387
  195.9 5.0 %collective-permute-start.20 = (bf16[33,32,128]{2,1,0:T(8,128)(2,1)S(1)}, bf16[33,32,128]{2,1,0:T(8,128)(2,1)S(1)}, u32[]{:S(2)}, u32[]{:S(2)}) collective-permute-start(bf16[33,32,128]{2,1,0:T(8,128)(2,1)S(1)} %get-tuple-element.193.refs_13_), channel_id=1, source_target_pairs={{0,3},{1,0},{2,1},{3,2},{4,7},{5,4},{6,5},{7,6},{8,11},{9,8},{10,9... | collective-permute-start | bytes 811016 | tf_op jit(solution)/shard_map/ppermute | solution.py:387
  226.8 6.8 %tile_grads.2 = bf16[128,128,128]{2,1,0:T(8,128)(2,1)} custom-call(s32[4]{0:T(128)S(1)} %pad_add_fusion.refs_0_.tab, s32[512]{0:T(512)S(1)} %bitcast.86, s32[512]{0:T(512)S(1)} %bitcast.110, bf16[4,32,32,128]{3,2,1,0:T(8,128)(2,1)S(1)} %copy-done.8, bf16[4,32,32,128]{3,2,1,0:T(8,128)(2,1)S(1)} %collective-permute-done.23.refs_1_, ...), custom_call_target="tpu_custom_call" | custom-call | flops 1073741824 | bytes 25165824 | tf_op jit(solution)/shard_map/tile_grads/pallas_call | solution.py:332
  233.6 8.2 %all-to-all-start.1 = ((bf16[16,8,128,128]{3,2,1,0:T(8,128)(2,1)}), bf16[16,8,128,128]{3,2,1,0:T(8,128)(2,1)}, u32[]{:S(2)}, u32[]{:S(2)}) async-start(bf16[16,8,128,128]{3,2,1,0:T(8,128)(2,1)} %bitcast.118), calls=%async_computation.1 | async-start | bytes 8388608 | tf_op jit(solution)/shard_map/all_to_all | solution.py:436
  241.9 14.9 %collective-permute-done.26.refs_10_ = bf16[2,32,32,128]{3,2,1,0:T(8,128)(2,1)S(1)} collective-permute-done((bf16[2,32,32,128]{3,2,1,0:T(8,128)(2,1)S(1)}, bf16[2,32,32,128]{3,2,1,0:T(8,128)(2,1)S(1)}, u32[]{:S(2)}, u32[]{:S(2)}) %collective-permute-start.26) | collective-permute-done | bytes 524320 | tf_op jit(solution)/shard_map/ppermute | solution.py:387
  266.1 5.1 %collective-permute-done.27.refs_9_ = bf16[33,32,128]{2,1,0:T(8,128)(2,1)S(1)} collective-permute-done((bf16[33,32,128]{2,1,0:T(8,128)(2,1)S(1)}, bf16[33,32,128]{2,1,0:T(8,128)(2,1)S(1)}, u32[]{:S(2)}, u32[]{:S(2)}) %collective-permute-start.27) | collective-permute-done | bytes 270368 | tf_op jit(solution)/shard_map/ppermute | solution.py:387
  285.3 6.3 %collective-permute-done.30.refs_9_ = bf16[33,32,128]{2,1,0:T(8,128)(2,1)S(1)} collective-permute-done((bf16[33,32,128]{2,1,0:T(8,128)(2,1)S(1)}, bf16[33,32,128]{2,1,0:T(8,128)(2,1)S(1)}, u32[]{:S(2)}, u32[]{:S(2)}) %collective-permute-start.30) | collective-permute-done | bytes 270368 | tf_op jit(solution)/shard_map/ppermute | solution.py:387
  300.0 6.8 %tile_grads.3 = bf16[128,128,128]{2,1,0:T(8,128)(2,1)} custom-call(s32[4]{0:T(128)S(1)} %pad_add_fusion.refs_0_.tab, s32[512]{0:T(512)S(1)} %bitcast.91, s32[512]{0:T(512)S(1)} %bitcast.115, bf16[4,32,32,128]{3,2,1,0:T(8,128)(2,1)S(1)} %copy-done.5, bf16[4,32,32,128]{3,2,1,0:T(8,128)(2,1)S(1)} %collective-permute-done.8.refs_1_, ...), custom_call_target="tpu_custom_call" | custom-call | flops 1073741824 | bytes 25165824 | tf_op jit(solution)/shard_map/tile_grads/pallas_call | solution.py:332
  306.8 7.7 %all-to-all-start = ((bf16[16,8,128,128]{3,2,1,0:T(8,128)(2,1)}), bf16[16,8,128,128]{3,2,1,0:T(8,128)(2,1)}, u32[]{:S(2)}, u32[]{:S(2)}) async-start(bf16[16,8,128,128]{3,2,1,0:T(8,128)(2,1)} %bitcast.119), calls=%async_computation | async-start | bytes 8388608 | tf_op jit(solution)/shard_map/all_to_all | solution.py:436
  317.7 51.3 %all-to-all-done.given = bf16[16,8,128,128]{3,2,1,0:T(8,128)(2,1)} async-done(((bf16[16,8,128,128]{3,2,1,0:T(8,128)(2,1)}), bf16[16,8,128,128]{3,2,1,0:T(8,128)(2,1)}, u32[]{:S(2)}, u32[]{:S(2)}) %all-to-all-start) | async-done | bytes 4194336 | tf_op jit(solution)/shard_map/all_to_all | solution.py:436
  (186 shorter events, 160.6 us)
Async XLA Ops:
  14.2 10.4 %collective-permute-start = (bf16[33,32,128]{2,1,0:T(8,128)(2,1)S(1)}, bf16[33,32,128]{2,1,0:T(8,128)(2,1)S(1)}, u32[]{:S(2)}, u32[]{:S(2)}) collective-permute-start(bf16[33,32,128]{2,1,0:T(8,128)(2,1)S(1)} %get-tuple-element.115.refs_7_), channel_id=1, source_target_pairs={{0,1},{1,2},{2,3},{3,0},{4,5},{5,6},{6,7},{7,4},{8,9},{9,10},{10,1... | collective-permute-start | bytes 811016 | tf_op jit(solution)/shard_map/ppermute | solution.py:387
  28.6 8.9 %collective-permute-start.1 = (bf16[33,32,128]{2,1,0:T(8,128)(2,1)S(1)}, bf16[33,32,128]{2,1,0:T(8,128)(2,1)S(1)}, u32[]{:S(2)}, u32[]{:S(2)}) collective-permute-start(bf16[33,32,128]{2,1,0:T(8,128)(2,1)S(1)} %get-tuple-element.119), channel_id=1, source_target_pairs={{0,1},{1,2},{2,3},{3,0},{4,5},{5,6},{6,7},{7,4},{8,9},{9,10},{10,1... | collective-permute-start | bytes 811016 | tf_op jit(solution)/shard_map/ppermute | solution.py:387
  28.7 13.7 %collective-permute-start.3 = (bf16[2,32,32,128]{3,2,1,0:T(8,128)(2,1)S(1)}, bf16[2,32,32,128]{3,2,1,0:T(8,128)(2,1)S(1)}, u32[]{:S(2)}, u32[]{:S(2)}) collective-permute-start(bf16[2,32,32,128]{3,2,1,0:T(8,128)(2,1)S(1)} %get-tuple-element.127), channel_id=1, source_target_pairs={{0,3},{1,0},{2,1},{3,2},{4,7},{5,4},{6,5},{7,6},{8,11},{9,8},{10,9... | collective-permute-start | bytes 1572872 | tf_op jit(solution)/shard_map/ppermute | solution.py:387
  41.6 8.0 %collective-permute-start.2 = (bf16[33,32,128]{2,1,0:T(8,128)(2,1)S(1)}, bf16[33,32,128]{2,1,0:T(8,128)(2,1)S(1)}, u32[]{:S(2)}, u32[]{:S(2)}) collective-permute-start(bf16[33,32,128]{2,1,0:T(8,128)(2,1)S(1)} %get-tuple-element.126.refs_8_), channel_id=1, source_target_pairs={{0,1},{1,2},{2,3},{3,0},{4,5},{5,6},{6,7},{7,4},{8,9},{9,10},{10,1... | collective-permute-start | bytes 811016 | tf_op jit(solution)/shard_map/ppermute | solution.py:387
  53.7 7.7 %collective-permute-start.4 = (bf16[33,32,128]{2,1,0:T(8,128)(2,1)S(1)}, bf16[33,32,128]{2,1,0:T(8,128)(2,1)S(1)}, u32[]{:S(2)}, u32[]{:S(2)}) collective-permute-start(bf16[33,32,128]{2,1,0:T(8,128)(2,1)S(1)} %get-tuple-element.129), channel_id=1, source_target_pairs={{0,1},{1,2},{2,3},{3,0},{4,5},{5,6},{6,7},{7,4},{8,9},{9,10},{10,1... | collective-permute-start | bytes 811016 | tf_op jit(solution)/shard_map/ppermute | solution.py:387
  53.7 11.7 %collective-permute-start.6 = (bf16[2,32,32,128]{3,2,1,0:T(8,128)(2,1)S(1)}, bf16[2,32,32,128]{3,2,1,0:T(8,128)(2,1)S(1)}, u32[]{:S(2)}, u32[]{:S(2)}) collective-permute-start(bf16[2,32,32,128]{3,2,1,0:T(8,128)(2,1)S(1)} %get-tuple-element.132), channel_id=1, source_target_pairs={{0,3},{1,0},{2,1},{3,2},{4,7},{5,4},{6,5},{7,6},{8,11},{9,8},{10,9... | collective-permute-start | bytes 1572872 | tf_op jit(solution)/shard_map/ppermute | solution.py:387
  76.3 11.3 %collective-permute-start.10 = (bf16[2,32,32,128]{3,2,1,0:T(8,128)(2,1)S(1)}, bf16[2,32,32,128]{3,2,1,0:T(8,128)(2,1)S(1)}, u32[]{:S(2)}, u32[]{:S(2)}) collective-permute-start(bf16[2,32,32,128]{3,2,1,0:T(8,128)(2,1)S(1)} %get-tuple-element.144), channel_id=1, source_target_pairs={{0,3},{1,0},{2,1},{3,2},{4,7},{5,4},{6,5},{7,6},{8,11},{9,8},{10,9... | collective-permute-start | bytes 1572872 | tf_op jit(solution)/shard_map/ppermute | solution.py:387
  98.8 12.9 %collective-permute-start.13 = (bf16[2,32,32,128]{3,2,1,0:T(8,128)(2,1)S(1)}, bf16[2,32,32,128]{3,2,1,0:T(8,128)(2,1)S(1)}, u32[]{:S(2)}, u32[]{:S(2)}) collective-permute-start(bf16[2,32,32,128]{3,2,1,0:T(8,128)(2,1)S(1)} %get-tuple-element.151), channel_id=1, source_target_pairs={{0,3},{1,0},{2,1},{3,2},{4,7},{5,4},{6,5},{7,6},{8,11},{9,8},{10,9... | collective-permute-start | bytes 1572872 | tf_op jit(solution)/shard_map/ppermute | solution.py:387
  111.7 8.3 %collective-permute-start.12 = (bf16[33,32,128]{2,1,0:T(8,128)(2,1)S(1)}, bf16[33,32,128]{2,1,0:T(8,128)(2,1)S(1)}, u32[]{:S(2)}, u32[]{:S(2)}) collective-permute-start(bf16[33,32,128]{2,1,0:T(8,128)(2,1)S(1)} %get-tuple-element.150), channel_id=1, source_target_pairs={{0,1},{1,2},{2,3},{3,0},{4,5},{5,6},{6,7},{7,4},{8,9},{9,10},{10,1... | collective-permute-start | bytes 811016 | tf_op jit(solution)/shard_map/ppermute | solution.py:387
  142.2 10.7 %collective-permute-start.15 = (bf16[33,32,128]{2,1,0:T(8,128)(2,1)S(1)}, bf16[33,32,128]{2,1,0:T(8,128)(2,1)S(1)}, u32[]{:S(2)}, u32[]{:S(2)}) collective-permute-start(bf16[33,32,128]{2,1,0:T(8,128)(2,1)S(1)} %get-tuple-element.174.refs_10_), channel_id=1, source_target_pairs={{0,3},{1,0},{2,1},{3,2},{4,7},{5,4},{6,5},{7,6},{8,11},{9,8},{10,9... | collective-permute-start | bytes 811016 | tf_op jit(solution)/shard_map/ppermute | solution.py:387
  153.6 13.3 %collective-permute-start.16 = (bf16[33,32,128]{2,1,0:T(8,128)(2,1)S(1)}, bf16[33,32,128]{2,1,0:T(8,128)(2,1)S(1)}, u32[]{:S(2)}, u32[]{:S(2)}) collective-permute-start(bf16[33,32,128]{2,1,0:T(8,128)(2,1)S(1)} %get-tuple-element.176), channel_id=1, source_target_pairs={{0,3},{1,0},{2,1},{3,2},{4,7},{5,4},{6,5},{7,6},{8,11},{9,8},{10,9... | collective-permute-start | bytes 811016 | tf_op jit(solution)/shard_map/ppermute | solution.py:387
  161.3 14.1 %collective-permute-start.18 = (bf16[2,32,32,128]{3,2,1,0:T(8,128)(2,1)S(1)}, bf16[2,32,32,128]{3,2,1,0:T(8,128)(2,1)S(1)}, u32[]{:S(2)}, u32[]{:S(2)}) collective-permute-start(bf16[2,32,32,128]{3,2,1,0:T(8,128)(2,1)S(1)} %get-tuple-element.189), channel_id=1, source_target_pairs={{0,1},{1,2},{2,3},{3,0},{4,5},{5,6},{6,7},{7,4},{8,9},{9,10},{10,1... | collective-permute-start | bytes 1572872 | tf_op jit(solution)/shard_map/ppermute | solution.py:387
  167.7 12.5 %collective-permute-start.17 = (bf16[33,32,128]{2,1,0:T(8,128)(2,1)S(1)}, bf16[33,32,128]{2,1,0:T(8,128)(2,1)S(1)}, u32[]{:S(2)}, u32[]{:S(2)}) collective-permute-start(bf16[33,32,128]{2,1,0:T(8,128)(2,1)S(1)} %get-tuple-element.188.refs_11_), channel_id=1, source_target_pairs={{0,3},{1,0},{2,1},{3,2},{4,7},{5,4},{6,5},{7,6},{8,11},{9,8},{10,9... | collective-permute-start | bytes 811016 | tf_op jit(solution)/shard_map/ppermute | solution.py:387
  183.4 9.3 %collective-permute-start.19 = (bf16[33,32,128]{2,1,0:T(8,128)(2,1)S(1)}, bf16[33,32,128]{2,1,0:T(8,128)(2,1)S(1)}, u32[]{:S(2)}, u32[]{:S(2)}) collective-permute-start(bf16[33,32,128]{2,1,0:T(8,128)(2,1)S(1)} %get-tuple-element.191), channel_id=1, source_target_pairs={{0,3},{1,0},{2,1},{3,2},{4,7},{5,4},{6,5},{7,6},{8,11},{9,8},{10,9... | collective-permute-start | bytes 811016 | tf_op jit(solution)/shard_map/ppermute | solution.py:387
  188.7 12.2 %collective-permute-start.21 = (bf16[2,32,32,128]{3,2,1,0:T(8,128)(2,1)S(1)}, bf16[2,32,32,128]{3,2,1,0:T(8,128)(2,1)S(1)}, u32[]{:S(2)}, u32[]{:S(2)}) collective-permute-start(bf16[2,32,32,128]{3,2,1,0:T(8,128)(2,1)S(1)} %get-tuple-element.194), channel_id=1, source_target_pairs={{0,1},{1,2},{2,3},{3,0},{4,5},{5,6},{6,7},{7,4},{8,9},{9,10},{10,1... | collective-permute-start | bytes 1572872 | tf_op jit(solution)/shard_map/ppermute | solution.py:387
  195.9 9.0 %collective-permute-start.20 = (bf16[33,32,128]{2,1,0:T(8,128)(2,1)S(1)}, bf16[33,32,128]{2,1,0:T(8,128)(2,1)S(1)}, u32[]{:S(2)}, u32[]{:S(2)}) collective-permute-start(bf16[33,32,128]{2,1,0:T(8,128)(2,1)S(1)} %get-tuple-element.193.refs_13_), channel_id=1, source_target_pairs={{0,3},{1,0},{2,1},{3,2},{4,7},{5,4},{6,5},{7,6},{8,11},{9,8},{10,9... | collective-permute-start | bytes 811016 | tf_op jit(solution)/shard_map/ppermute | solution.py:387
  208.1 8.9 %collective-permute-start.22 = (bf16[33,32,128]{2,1,0:T(8,128)(2,1)S(1)}, bf16[33,32,128]{2,1,0:T(8,128)(2,1)S(1)}, u32[]{:S(2)}, u32[]{:S(2)}) collective-permute-start(bf16[33,32,128]{2,1,0:T(8,128)(2,1)S(1)} %get-tuple-element.197), channel_id=1, source_target_pairs={{0,3},{1,0},{2,1},{3,2},{4,7},{5,4},{6,5},{7,6},{8,11},{9,8},{10,9... | collective-permute-start | bytes 811016 | tf_op jit(solution)/shard_map/ppermute | solution.py:387
  213.1 12.4 %collective-permute-start.23 = (bf16[4,32,32,128]{3,2,1,0:T(8,128)(2,1)S(1)}, bf16[4,32,32,128]{3,2,1,0:T(8,128)(2,1)S(1)}, u32[]{:S(2)}, u32[]{:S(2)}) collective-permute-start(bf16[4,32,32,128]{3,2,1,0:T(8,128)(2,1)S(1)} %copy-done.8), channel_id=1, source_target_pairs={{0,4},{4,0},{8,12},{12,8},{16,20},{20,16},{24,28},{28,24},{32,36},... | collective-permute-start | bytes 3145736 | tf_op jit(solution)/shard_map/ppermute | solution.py:432
  220.6 13.0 %collective-permute-start.25 = (bf16[33,32,128]{2,1,0:T(8,128)(2,1)S(1)}, bf16[33,32,128]{2,1,0:T(8,128)(2,1)S(1)}, u32[]{:S(2)}, u32[]{:S(2)}) collective-permute-start(bf16[33,32,128]{2,1,0:T(8,128)(2,1)S(1)} %get-tuple-element.212.refs_11_), channel_id=1, source_target_pairs={{0,3},{1,0},{2,1},{3,2},{4,7},{5,4},{6,5},{7,6},{8,11},{9,8},{10,9... | collective-permute-start | bytes 811016 | tf_op jit(solution)/shard_map/ppermute | solution.py:387
  233.6 73.3 %all-to-all-start.1 = ((bf16[16,8,128,128]{3,2,1,0:T(8,128)(2,1)}), bf16[16,8,128,128]{3,2,1,0:T(8,128)(2,1)}, u32[]{:S(2)}, u32[]{:S(2)}) async-start(bf16[16,8,128,128]{3,2,1,0:T(8,128)(2,1)} %bitcast.118), calls=%async_computation.1 | async-start | bytes 8388608 | tf_op jit(solution)/shard_map/all_to_all | solution.py:436
  241.8 15.0 %collective-permute-start.26 = (bf16[2,32,32,128]{3,2,1,0:T(8,128)(2,1)S(1)}, bf16[2,32,32,128]{3,2,1,0:T(8,128)(2,1)S(1)}, u32[]{:S(2)}, u32[]{:S(2)}) collective-permute-start(bf16[2,32,32,128]{3,2,1,0:T(8,128)(2,1)S(1)} %get-tuple-element.214), channel_id=1, source_target_pairs={{0,1},{1,2},{2,3},{3,0},{4,5},{5,6},{6,7},{7,4},{8,9},{9,10},{10,1... | collective-permute-start | bytes 1572872 | tf_op jit(solution)/shard_map/ppermute | solution.py:387
  266.1 13.9 %collective-permute-start.29 = (bf16[2,32,32,128]{3,2,1,0:T(8,128)(2,1)S(1)}, bf16[2,32,32,128]{3,2,1,0:T(8,128)(2,1)S(1)}, u32[]{:S(2)}, u32[]{:S(2)}) collective-permute-start(bf16[2,32,32,128]{3,2,1,0:T(8,128)(2,1)S(1)} %get-tuple-element.219), channel_id=1, source_target_pairs={{0,1},{1,2},{2,3},{3,0},{4,5},{5,6},{6,7},{7,4},{8,9},{9,10},{10,1... | collective-permute-start | bytes 1572872 | tf_op jit(solution)/shard_map/ppermute | solution.py:387
  285.2 10.8 %collective-permute-start.8 = (bf16[4,32,32,128]{3,2,1,0:T(8,128)(2,1)S(1)}, bf16[4,32,32,128]{3,2,1,0:T(8,128)(2,1)S(1)}, u32[]{:S(2)}, u32[]{:S(2)}) collective-permute-start(bf16[4,32,32,128]{3,2,1,0:T(8,128)(2,1)S(1)} %copy-done.5), channel_id=1, source_target_pairs={{0,4},{4,0},{8,12},{12,8},{16,20},{20,16},{24,28},{28,24},{32,36},... | collective-permute-start | bytes 3145736 | tf_op jit(solution)/shard_map/ppermute | solution.py:432
  306.8 62.2 %all-to-all-start = ((bf16[16,8,128,128]{3,2,1,0:T(8,128)(2,1)}), bf16[16,8,128,128]{3,2,1,0:T(8,128)(2,1)}, u32[]{:S(2)}, u32[]{:S(2)}) async-start(bf16[16,8,128,128]{3,2,1,0:T(8,128)(2,1)} %bitcast.119), calls=%async_computation | async-start | bytes 8388608 | tf_op jit(solution)/shard_map/all_to_all | solution.py:436
  (66 other events, 1003.8 us)
where the time goes:
time: 374 us; the launch traced here: 373 us
  waiting for transfers between devices  180 us (48%)
  Pallas kernels  94.8 us (25%)
  starting transfers between devices  76.6 us (20%)
  local copies, waits for them, and re-layouts  18.9 us (5%)
    ppermute x28, waiting for transfers between devices, ring(): lax.ppermute(part, 'section', [(i, (i + by) % sections) for i in range(se...  126 us
    pallas_call x22, Pallas kernels, tick_call(): pl.pallas_call(kernel, in_specs=[SM] * 3 + [VM] * (len(names) - 3 + len(p...  75 us
    ppermute x28, starting transfers between devices, ring(): lax.ppermute(part, 'section', [(i, (i + by) % sections) for i in range(se...  60.2 us
    all_to_all x2, waiting for transfers between devices, trade(): lax.all_to_all(part.reshape(chips, share, tile, tile), 'dp', 0, 0, axis_i...  51.3 us
    unnamed x112, local copies, waits for them, and re-layouts  18.9 us
    all_to_all x2, starting transfers between devices, trade(): lax.all_to_all(part.reshape(chips, share, tile, tile), 'dp', 0, 0, axis_i...  15.9 us
    pallas_call x2, Pallas kernels, tile_grads(): pl.pallas_call(kernel, grid_spec=pltpu.PrefetchScalarGridSpec(num_scalar_...  13.5 us
  transfers between devices with their start and end apart: 34, of which 25 were waited for; matrix products, arithmetic and copies ran while one was open for 0% of the time, Pallas kernels for 15%

commit v1 on v0

--- a/solution.py
+++ b/solution.py
@@ -16,7 +16,8 @@
 SM = pl.BlockSpec(memory_space=pltpu.SMEM)
 HBM = pl.BlockSpec(memory_space=pltpu.HBM)
 LIMIT = 10 * 2**20
-GRAD_LIMIT = 12 * 2**20
+GRAD_LIMIT = 9 * 2**20
+PARTS = 2
 
 
 def split_pair(value, width):
@@ -74,7 +75,7 @@
     first_turn = 0 if forward else 1
     turns_here = [first_turn] * use_entering + [1 - first_turn] * use_prev
     critical, early = "critical" in named, "early" in named
-    early_at = (order - plan.span) % plan.bundle
+    early_at = (order - plan.span - 1) % plan.bundle
     saves = ["kept", "slope", "scale"] if forward else ["grad"]
     piece = tick if tick < plan.span else tick - plan.turns * M
     turning = forward and (tick < plan.span or tick >= plan.turns * M)
@@ -86,16 +87,19 @@
         shape, kind = ((T, B), f32) if name == "scale" else ((G, T, B), bf16)
         shapes[name + "_out"] = (HBM, jax.ShapeDtypeStruct(shape, kind) if last else pltpu.HBM(shape, kind))
     alias_from = {}
-    for turn in turns_here:
-        shapes["store%d" % turn] = (HBM, pltpu.HBM((M, G, T, B), bf16))
-        if stores[turn] is not None:
-            alias_from["store%d" % turn] = stores[turn]
+    slots_of = ["store%d" % turn for turn in turns_here]
+    for name in slots_of:
+        shapes[name] = (HBM, pltpu.HBM((M, G, T, B), bf16))
+        if name in stores:
+            alias_from[name] = stores[name]
     if turning:
         for turn in range(2):
             shapes["turned%d" % turn] = (HBM, pltpu.HBM((plan.slots, B, B), bf16))
             if turned[turn] is not None:
                 alias_from["turned%d" % turn] = turned[turn]
-    if pack:
+    packs = pack is not None
+    pack = pack or ()
+    if packs:
         shapes["bundle"] = (VM, jax.ShapeDtypeStruct((plan.bundle, G, T, B), bf16))
     out_names = list(shapes)
     scratch = {"source": pltpu.VMEM((G, T, B), bf16), "acc": pltpu.VMEM((G + 1, T, B), f32)}
@@ -106,7 +110,7 @@
     if forward and tick < M:
         scratch["extra"] = pltpu.VMEM((T, B), f32)
     scratch["sems"] = pltpu.SemaphoreType.DMA((5,))
-    if pack:
+    if packs:
         scratch["pack_sems"] = pltpu.SemaphoreType.DMA((plan.bundle,))
 
     def kernel(*refs):
@@ -120,7 +124,7 @@
         active = (step >= 0) & (step < 2 * M)
         parity = tab[plan.section] % 2
         entry = (parity if forward else 1 - parity) * (G * B)
-        packing = [pltpu.make_async_copy(old.at[pl.ds(0, G)], out["bundle"].at[i], own["pack_sems"].at[i]) for i, old in enumerate(pack and older_sent)]
+        packing = [pltpu.make_async_copy(old.at[pl.ds(0, G)], out["bundle"].at[i], own["pack_sems"].at[i]) for i, old in enumerate(older_sent)]
         for copy in packing:
             copy.start()
 
@@ -138,14 +142,14 @@
 
         def send(b, value):
             sent[b] = value
-            if pack:
+            if packs:
                 out["bundle"][plan.bundle - 1, b] = value
 
         def keep(turn, unit, copies):
-            for place in turns_here:
+            for place, name in zip(turns_here, slots_of):
                 @pl.when(turn == place)
                 def _():
-                    pltpu.make_async_copy(source, out["store%d" % place].at[unit], sems.at[0]).start()
+                    pltpu.make_async_copy(source, out[name].at[unit], sems.at[0]).start()
             for copy in copies:
                 copy.start()
             acc[...] = jnp.zeros_like(acc)
@@ -253,14 +257,14 @@
 
                 each_block(G, leave)
                 sent[G] = split_pair(factor, B)
-            pltpu.make_async_copy(source, out["store%d" % turns_here[0]].at[unit], sems.at[0]).wait()
+            pltpu.make_async_copy(source, out[slots_of[0]].at[unit], sems.at[0]).wait()
             for copy in copies:
                 copy.wait()
 
         @pl.when(jnp.logical_not(active))
         def _():
             sent[...] = jnp.zeros_like(sent)
-            if pack:
+            if packs:
                 out["bundle"][plan.bundle - 1] = jnp.zeros((G, T, B), bf16)
             if turning:
                 flipped = own["flipped"]
@@ -297,7 +301,7 @@
     return dict(zip(out_names, outs))
 
 
-def tile_grads(plan, turn, info, rows, cols, normed_pair, error_pair, share, parts):
+def tile_grads(plan, turn, info, rows, cols, normed_parts, error_parts, share, parts):
     G, T, B, M = plan.grid, plan.rows, plan.tile, plan.units
     local = plan.slots // parts
     steps = 8
@@ -306,7 +310,7 @@
 
     def kernel(tab, rows_at, cols_at, *refs):
         normeds, errors = refs[:parts], refs[parts:2 * parts]
-        out, turned, flat = refs[2 * parts:]
+        out, turned, flat = refs[-3:]
         step = pl.program_id(0)
 
         @pl.when(step == 0)
@@ -342,7 +346,7 @@
         compiler_params=pltpu.CompilerParams(vmem_limit_bytes=GRAD_LIMIT),
         cost_estimate=pl.CostEstimate(flops=2 * local * B * B * parts * tokens, transcendentals=0, bytes_accessed=24 * 2**20),
         name="tile_grads",
-    )(info, rows, cols, *normed_pair, *error_pair)
+    )(info, rows, cols, *normed_parts, *error_parts)
 
 
 def sum_parts(parts):
@@ -355,9 +359,9 @@
     rest = parts.shape[2:]
     return pl.pallas_call(
         kernel,
-        grid=(parts.shape[1] // 2,),
-        in_specs=[pl.BlockSpec((parts.shape[0], 2, *rest), lambda i: (0, i, 0, 0))],
-        out_specs=pl.BlockSpec((2, *rest), lambda i: (i, 0, 0)),
+        grid=(parts.shape[1],),
+        in_specs=[pl.BlockSpec((parts.shape[0], 1, *rest), lambda i: (0, i, 0, 0))],
+        out_specs=pl.BlockSpec((1, *rest), lambda i: (i, 0, 0)),
         out_shape=jax.ShapeDtypeStruct(parts.shape[1:], bf16),
         compiler_params=pltpu.CompilerParams(vmem_limit_bytes=GRAD_LIMIT),
         name="sum_parts",
@@ -368,7 +372,7 @@
     sections = lax.axis_size("section")
     replicas = lax.axis_size("dp")
     section_pos = lax.axis_index("section").astype(jnp.int32)
-    core = (lax.axis_index("dp") % 2).astype(jnp.int32)
+    core = (lax.axis_index("dp") % PARTS).astype(jnp.int32)
     turns, slots, tile = blocks.shape[0], blocks.shape[2], blocks.shape[3]
     tokens = hidden_in.shape[0] * hidden_in.shape[1]
     half_width = hidden_in.shape[2] // 2
@@ -387,7 +391,7 @@
         return lax.ppermute(part, "section", [(i, (i + by) % sections) for i in range(sections)])
 
     def run(forward, weights, saved, hook):
-        stores, turned = [None, None], [None, None]
+        stores, turned = {}, [None, None]
         sents, ahead, bundles, kept = [], [], {}, []
         toward = 1 if forward else -1
         for order in range(plan.ticks):
@@ -406,48 +410,49 @@
                 named["kept"], named["slope"], named["scale"] = [saved[tick][name + "_out"] for name in ("kept", "slope", "scale")]
                 named["prev"] = kept[order - M]["grad_out"] if use_prev else None
             named["critical"] = ahead[order - LAG] if order >= LAG else None
-            named["early"] = bundles[(order - plan.span) // plan.bundle] if order >= plan.span else None
-            pack = ()
-            if order % plan.bundle == plan.bundle - 1 and order - plan.bundle + 1 + plan.span < plan.ticks:
-                pack = tuple(sents[order - plan.bundle + 1:order])
+            named["early"] = bundles[-(-(order - plan.span) // plan.bundle)] if order >= plan.span else None
+            pack = None
+            if order % plan.bundle == 0 and order - plan.bundle + 1 + plan.span < plan.ticks:
+                pack = tuple(sents[max(order - plan.bundle + 1, 0):order])
             made = tick_call(plan, tick, order, forward, named, stores, pack, turned, order == plan.ticks - 1)
             sents.append(made["sent"])
             kept.append(made)
-            stores = [made.get("store%d" % turn, stores[turn]) for turn in range(2)]
+            stores = stores | {name: made[name] for name in ("store0", "store1") if name in made}
             turned = [made.get("turned%d" % turn, turned[turn]) for turn in range(2)]
             ahead.append(ring(made["sent"], toward) if order + LAG < plan.ticks else None)
-            if pack:
+            if pack is not None:
                 bundles[order // plan.bundle] = ring(made["bundle"], -toward)
             hook(order, ahead, stores)
         return kept, stores, turned
 
     saved, normed, turned = run(True, weights, None, lambda order, ahead, stores: None)
 
-    chips = replicas // 2
-    swap = [(i, i ^ 1) for i in range(replicas)]
+    members = replicas // PARTS
     share = slots // replicas
-    same_core = [[i for i in range(replicas) if i % 2 == c] for c in range(2)]
-
-    def make_grads(turn, error):
-        pairs = [[own, lax.ppermute(own, "dp", swap)] for own in (normed[turn], error)]
-        return tile_grads(plan, turn, info, rows, cols, pairs[0], pairs[1], share, 2)
+    alike = [[i for i in range(replicas) if i % PARTS == q] for q in range(PARTS)]
+
+    def gather(own):
+        return [own, lax.ppermute(own, "dp", [(i, i ^ 1) for i in range(replicas)])]
+
+    def make_grads(turn, stores):
+        name = "store%d" % turn
+        return tile_grads(plan, turn, info, rows, cols, gather(normed[name]), gather(stores[name]), share, PARTS)
 
     def trade(part):
         return lax.all_to_all(
-            part.reshape(chips, share, tile, tile), "dp", 0, 0, axis_index_groups=same_core, tiled=True
+            part.reshape(members, share, tile, tile), "dp", 0, 0, axis_index_groups=alike, tiled=True
         )
 
     later = []
 
     def halfway(order, ahead, stores):
         if order == M + plan.span - 1:
-            part, ahead[order] = lax.optimization_barrier((make_grads(1, stores[1]), ahead[order]))
-            later.append(trade(part))
+            part, ahead[order] = lax.optimization_barrier((make_grads(1, stores), ahead[order]))
+            later.append(lax.psum_scatter(part, "dp", scatter_dimension=0, axis_index_groups=alike, tiled=True))
 
     _, errors, _ = run(False, turned, saved, halfway)
-    sooner = trade(make_grads(0, errors[0]))
-    results = [sum_parts(sooner), sum_parts(later[0])]
-    return jnp.stack(results)[:, None]
+    sooner = trade(make_grads(0, errors))
+    return jnp.stack([sum_parts(sooner), later[0]])[:, None]
 
 
 def solution(mesh):

time: 374 us -> 369 us (0.987)
  blocking collectives: 0 us -> 63.6 us
  waiting for transfers between devices: 180 us -> 117 us
  starting transfers between devices: 76.6 us -> 46.1 us
  between operations: 0.72 us -> 14.2 us
  Pallas kernels: 94.8 us -> 107 us
    all_to_all x0 -> x1, blocking collectives: none -> 63.6 us  [trade(): lax.all_to_all(part.reshape(members, share, tile, tile), 'dp', 0, 0, axis...]
    all_to_all x2 -> x0, waiting for transfers between devices: 51.3 us -> none  [trade(): lax.all_to_all(part.reshape(chips, share, tile, tile), 'dp', 0, 0, axis_i...]
    pallas_call x22, Pallas kernels: 75 us -> 92.7 us  [tick_call(): pl.pallas_call(kernel, in_specs=[SM] * 3 + [VM] * (len(names) - 3 + len(p...]
    all_to_all x2 -> x0, starting transfers between devices: 15.9 us -> none  [trade(): lax.all_to_all(part.reshape(chips, share, tile, tile), 'dp', 0, 0, axis_i...]
    ppermute x28 -> x30, waiting for transfers between devices: 126 us -> 112 us  [ring(): lax.ppermute(part, 'section', [(i, (i + by) % sections) for i in range(se...]
    ppermute x28 -> x30, starting transfers between devices: 60.2 us -> 45.9 us  [ring(): lax.ppermute(part, 'section', [(i, (i + by) % sections) for i in range(se...]
    pallas_call x2 -> x1, Pallas kernels: 6.3 us -> 0.96 us  [sum_parts(): pl.pallas_call(kernel, grid=(parts.shape[1],), in_specs=[pl.BlockSpec((pa...]
  transfers between devices with their start and end apart: 34 -> 35, of which waited for: 25 -> 25; matrix products, arithmetic and copies ran while one was open for 0% -> 0% of each run, Pallas kernels for 15% -> 19%
where the time goes in v1:
time: 369 us; the launch traced here: 370 us
  waiting for transfers between devices  117 us (32%)
  Pallas kernels  107 us (29%)
  blocking collectives  63.6 us (17%)
  starting transfers between devices  46.1 us (12%)
  local copies, waits for them, and re-layouts  18.9 us (5%)
  between operations  14.2 us (4%)
    ppermute x30, waiting for transfers between devices, ring(): lax.ppermute(part, 'section', [(i, (i + by) % sections) for i in range(se...  112 us
    pallas_call x22, Pallas kernels, tick_call(): pl.pallas_call(kernel, in_specs=[SM] * 3 + [VM] * (len(names) - 3 + len(p...  92.7 us
    all_to_all x1, blocking collectives, trade(): lax.all_to_all(part.reshape(members, share, tile, tile), 'dp', 0, 0, axis...  63.6 us
    ppermute x30, starting transfers between devices, ring(): lax.ppermute(part, 'section', [(i, (i + by) % sections) for i in range(se...  45.9 us
    unnamed x112, local copies, waits for them, and re-layouts  18.9 us
    pallas_call x2, Pallas kernels, tile_grads(): pl.pallas_call(kernel, grid_spec=pltpu.PrefetchScalarGridSpec(num_scalar_...  13.6 us
  transfers between devices with their start and end apart: 35, of which 25 were waited for; matrix products, arithmetic and copies ran while one was open for 0% of the time, Pallas kernels for 19%

profile of v1, /device:TPU:0, one launch (start us, length us, event | category | flops | bytes accessed | tf_op | source)
XLA Modules:
  0.0 369.6 jit_solution(1488053417637339919)
XLA Ops:
  7.3 5.8 %copy-done = bf16[2,1,256,128,128]{4,3,2,1,0:T(8,128)(2,1)S(1)} copy-done((bf16[2,1,256,128,128]{4,3,2,1,0:T(8,128)(2,1)S(1)}, bf16[2,1,256,128,128]{4,3,2,1,0:T(8,128)(2,1)}, u32[]{:S(2)}) %copy-start) | copy-done | bytes 16777240
  23.4 7.7 %collective-permute-done.refs_6_ = bf16[33,32,128]{2,1,0:T(8,128)(2,1)S(1)} collective-permute-done((bf16[33,32,128]{2,1,0:T(8,128)(2,1)S(1)}, bf16[33,32,128]{2,1,0:T(8,128)(2,1)S(1)}, u32[]{:S(2)}, u32[]{:S(2)}) %collective-permute-start) | collective-permute-done | bytes 270368 | tf_op jit(solution)/shard_map/ppermute | solution.py:391
  38.9 5.6 %collective-permute-done.1.refs_6_ = bf16[33,32,128]{2,1,0:T(8,128)(2,1)S(1)} collective-permute-done((bf16[33,32,128]{2,1,0:T(8,128)(2,1)S(1)}, bf16[33,32,128]{2,1,0:T(8,128)(2,1)S(1)}, u32[]{:S(2)}, u32[]{:S(2)}) %collective-permute-start.1) | collective-permute-done | bytes 270368 | tf_op jit(solution)/shard_map/ppermute | solution.py:391
  61.8 7.5 %collective-permute-done.4.refs_7_ = bf16[33,32,128]{2,1,0:T(8,128)(2,1)S(1)} collective-permute-done((bf16[33,32,128]{2,1,0:T(8,128)(2,1)S(1)}, bf16[33,32,128]{2,1,0:T(8,128)(2,1)S(1)}, u32[]{:S(2)}, u32[]{:S(2)}) %collective-permute-start.4) | collective-permute-done | bytes 270368 | tf_op jit(solution)/shard_map/ppermute | solution.py:391
  69.3 5.2 %forward_tick.15 = (bf16[33,32,128]{2,1,0:T(8,128)(2,1)S(1)}, bf16[32,32,128]{2,1,0:T(8,128)(2,1)}, bf16[32,32,128]{2,1,0:T(8,128)(2,1)}, f32[32,128]{1,0:T(8,12...) custom-call(s32[4]{0:T(128)S(1)} %pad_add_fusion.refs_0_.tab, ...), custom_call_target="tpu_custom_call", output_to_operand_aliasing={{4}: (10, {})} | custom-call | tf_op jit(solution)/shard_map/forward_tick/pallas_call | solution.py:291
  82.3 5.1 %forward_tick.16 = (bf16[33,32,128]{2,1,0:T(8,128)(2,1)S(1)}, bf16[32,32,128]{2,1,0:T(8,128)(2,1)}, bf16[32,32,128]{2,1,0:T(8,128)(2,1)}, f32[32,128]{1,0:T(8,12...) custom-call(s32[4]{0:T(128)S(1)} %pad_add_fusion.refs_0_.tab, ...), custom_call_target="tpu_custom_call", output_to_operand_aliasing={{4}: (9, {}), {5}: (10, {})} | custom-call | tf_op jit(solution)/shard_map/forward_tick/pallas_call | solution.py:291
  87.6 7.6 %collective-permute-done.7.refs_7_ = bf16[33,32,128]{2,1,0:T(8,128)(2,1)S(1)} collective-permute-done((bf16[33,32,128]{2,1,0:T(8,128)(2,1)S(1)}, bf16[33,32,128]{2,1,0:T(8,128)(2,1)S(1)}, u32[]{:S(2)}, u32[]{:S(2)}) %collective-permute-start.7) | collective-permute-done | bytes 270368 | tf_op jit(solution)/shard_map/ppermute | solution.py:391
  95.2 5.2 %forward_tick.17 = (bf16[33,32,128]{2,1,0:T(8,128)(2,1)S(1)}, bf16[32,32,128]{2,1,0:T(8,128)(2,1)}, bf16[32,32,128]{2,1,0:T(8,128)(2,1)}, f32[32,128]{1,0:T(8,12...) custom-call(s32[4]{0:T(128)S(1)} %pad_add_fusion.refs_0_.tab, ...), custom_call_target="tpu_custom_call", output_to_operand_aliasing={{4}: (10, {}), {5}: (11, {})} | custom-call | tf_op jit(solution)/shard_map/forward_tick/pallas_call | solution.py:291
  108.2 5.1 %forward_tick.18 = (bf16[33,32,128]{2,1,0:T(8,128)(2,1)S(1)}, bf16[32,32,128]{2,1,0:T(8,128)(2,1)}, bf16[32,32,128]{2,1,0:T(8,128)(2,1)}, f32[32,128]{1,0:T(8,128)}, bf16[4,32,32,128]{3,2,1,0:T(8,128)(2,1)}) custom-call(s32[4]{0:T(128)S(1)} %pad_add_fusion.refs_0_.tab, s32[512]{0:T(512)S(1)} %bitcast.74, ...), custom_call_target="tpu_custom_call", output_to_operand_aliasing={{4}: (8, {})} | custom-call | tf_op jit(solution)/shard_map/forward_tick/pallas_call | solution.py:291
  113.4 7.6 %collective-permute-done.11.refs_6_ = bf16[33,32,128]{2,1,0:T(8,128)(2,1)S(1)} collective-permute-done((bf16[33,32,128]{2,1,0:T(8,128)(2,1)S(1)}, bf16[33,32,128]{2,1,0:T(8,128)(2,1)S(1)}, u32[]{:S(2)}, u32[]{:S(2)}) %collective-permute-start.11) | collective-permute-done | bytes 270368 | tf_op jit(solution)/shard_map/ppermute | solution.py:391
  121.0 5.2 %forward_tick.19 = (bf16[33,32,128]{2,1,0:T(8,128)(2,1)S(1)}, bf16[32,32,128]{2,1,0:T(8,128)(2,1)}, bf16[32,32,128]{2,1,0:T(8,128)(2,1)}, f32[32,128]{1,0:T(8,12...) custom-call(s32[4]{0:T(128)S(1)} %pad_add_fusion.refs_0_.tab, ...), custom_call_target="tpu_custom_call", output_to_operand_aliasing={{4}: (9, {}), {5}: (10, {}), {6}: (11, {})} | custom-call | tf_op jit(solution)/shard_map/forward_tick/pallas_call | solution.py:291
  139.6 7.6 %collective-permute-done.14.refs_6_ = bf16[33,32,128]{2,1,0:T(8,128)(2,1)S(1)} collective-permute-done((bf16[33,32,128]{2,1,0:T(8,128)(2,1)S(1)}, bf16[33,32,128]{2,1,0:T(8,128)(2,1)S(1)}, u32[]{:S(2)}, u32[]{:S(2)}) %collective-permute-start.14) | collective-permute-done | bytes 270368 | tf_op jit(solution)/shard_map/ppermute | solution.py:391
  147.3 5.4 %forward_tick.21 = (bf16[33,32,128]{2,1,0:T(8,128)(2,1)}, bf16[32,32,128]{2,1,0:T(8,128)(2,1)S(1)}, bf16[32,32,128]{2,1,0:T(8,128)(2,1)S(1)}, f32[32,128]{1,0:T(...) custom-call(s32[4]{0:T(128)S(1)} %pad_add_fusion.refs_0_.tab, ...), custom_call_target="tpu_custom_call", output_to_operand_aliasing={{4}: (8, {}), {5}: (9, {}), {6}: (10, {})} | custom-call | tf_op jit(solution)/shard_map/forward_tick/pallas_call | solution.py:291
  159.1 6.2 %collective-permute-done.16.refs_9_ = bf16[33,32,128]{2,1,0:T(8,128)(2,1)S(1)} collective-permute-done((bf16[33,32,128]{2,1,0:T(8,128)(2,1)S(1)}, bf16[33,32,128]{2,1,0:T(8,128)(2,1)S(1)}, u32[]{:S(2)}, u32[]{:S(2)}) %collective-permute-start.16) | collective-permute-done | bytes 270368 | tf_op jit(solution)/shard_map/ppermute | solution.py:391
  166.0 7.0 %collective-permute-start.17 = (bf16[33,32,128]{2,1,0:T(8,128)(2,1)S(1)}, bf16[33,32,128]{2,1,0:T(8,128)(2,1)S(1)}, u32[]{:S(2)}, u32[]{:S(2)}) collective-permute-start(bf16[33,32,128]{2,1,0:T(8,128)(2,1)S(1)} %get-tuple-element.179.refs_10_), channel_id=1, source_target_pairs={{0,3},{1,0},{2,1},{3,2},{4,7},{5,4},{6,5},{7,6},{8,11},{9,8},{10,9... | collective-permute-start | bytes 811016 | tf_op jit(solution)/shard_map/ppermute | solution.py:391
  173.0 5.5 %collective-permute-done.17.refs_9_ = bf16[33,32,128]{2,1,0:T(8,128)(2,1)S(1)} collective-permute-done((bf16[33,32,128]{2,1,0:T(8,128)(2,1)S(1)}, bf16[33,32,128]{2,1,0:T(8,128)(2,1)S(1)}, u32[]{:S(2)}, u32[]{:S(2)}) %collective-permute-start.17) | collective-permute-done | bytes 270368 | tf_op jit(solution)/shard_map/ppermute | solution.py:391
  179.3 6.9 %collective-permute-start.18 = (bf16[33,32,128]{2,1,0:T(8,128)(2,1)S(1)}, bf16[33,32,128]{2,1,0:T(8,128)(2,1)S(1)}, u32[]{:S(2)}, u32[]{:S(2)}) collective-permute-start(bf16[33,32,128]{2,1,0:T(8,128)(2,1)S(1)} %get-tuple-element.191), channel_id=1, source_target_pairs={{0,3},{1,0},{2,1},{3,2},{4,7},{5,4},{6,5},{7,6},{8,11},{9,8},{10,9... | collective-permute-start | bytes 811016 | tf_op jit(solution)/shard_map/ppermute | solution.py:391
  219.7 5.5 %collective-permute-done.23.refs_11_ = bf16[33,32,128]{2,1,0:T(8,128)(2,1)S(1)} collective-permute-done((bf16[33,32,128]{2,1,0:T(8,128)(2,1)S(1)}, bf16[33,32,128]{2,1,0:T(8,128)(2,1)S(1)}, u32[]{:S(2)}, u32[]{:S(2)}) %collective-permute-start.23) | collective-permute-done | bytes 270368 | tf_op jit(solution)/shard_map/ppermute | solution.py:391
  225.3 5.7 %backward_tick.17 = (bf16[33,32,128]{2,1,0:T(8,128)(2,1)}, bf16[32,32,128]{2,1,0:T(8,128)(2,1)}, bf16[4,32,32,128]{3,2,1,0:T(8,128)(2,1)}, bf16[4,32,32,128]{3,2,1,0:T(8,128)(2,1)}, bf16[2,32,32,128]{3,2,1,0:T(8,128)(2,1)S(1)}) custom-call(s32[4]{0:T(128)S(1)} %pad_add_fusion.refs_0_.tab, ...), custom_call_target="tpu_custom_call", output_to_operand_aliasing={{2}: (14, {}), {3}: (15, {})} | custom-call | tf_op jit(solution)/shard_map/backward_tick/pallas_call | solution.py:291
  235.2 6.8 %tile_grads.2 = bf16[128,128,128]{2,1,0:T(8,128)(2,1)} custom-call(s32[4]{0:T(128)S(1)} %pad_add_fusion.refs_0_.tab, s32[512]{0:T(512)S(1)} %bitcast.85, s32[512]{0:T(512)S(1)} %bitcast.109, bf16[4,32,32,128]{3,2,1,0:T(8,128)(2,1)S(1)} %copy-done.5, bf16[4,32,32,128]{3,2,1,0:T(8,128)(2,1)S(1)} %collective-permute-done.25.refs_1_, ...), custom_call_target="tpu_custom_call" | custom-call | flops 1073741824 | bytes 25165824 | tf_op jit(solution)/shard_map/tile_grads/pallas_call | solution.py:336
  251.6 5.7 %collective-permute-done.29.refs_10_ = bf16[2,32,32,128]{3,2,1,0:T(8,128)(2,1)S(1)} collective-permute-done((bf16[2,32,32,128]{3,2,1,0:T(8,128)(2,1)S(1)}, bf16[2,32,32,128]{3,2,1,0:T(8,128)(2,1)S(1)}, u32[]{:S(2)}, u32[]{:S(2)}) %collective-permute-start.29) | collective-permute-done | bytes 524320 | tf_op jit(solution)/shard_map/ppermute | solution.py:391
  264.2 5.6 %collective-permute-done.30.refs_9_ = bf16[33,32,128]{2,1,0:T(8,128)(2,1)S(1)} collective-permute-done((bf16[33,32,128]{2,1,0:T(8,128)(2,1)S(1)}, bf16[33,32,128]{2,1,0:T(8,128)(2,1)S(1)}, u32[]{:S(2)}, u32[]{:S(2)}) %collective-permute-start.30) | collective-permute-done | bytes 270368 | tf_op jit(solution)/shard_map/ppermute | solution.py:391
  289.6 6.8 %tile_grads.3 = bf16[128,128,128]{2,1,0:T(8,128)(2,1)} custom-call(s32[4]{0:T(128)S(1)} %pad_add_fusion.refs_0_.tab, s32[512]{0:T(512)S(1)} %bitcast.90, s32[512]{0:T(512)S(1)} %bitcast.114, bf16[4,32,32,128]{3,2,1,0:T(8,128)(2,1)S(1)} %copy-done.6, bf16[4,32,32,128]{3,2,1,0:T(8,128)(2,1)S(1)} %collective-permute-done.9.refs_1_, ...), custom_call_target="tpu_custom_call" | custom-call | flops 1073741824 | bytes 25165824 | tf_op jit(solution)/shard_map/tile_grads/pallas_call | solution.py:336
  296.3 63.6 %all_to_all.5.given = bf16[16,8,128,128]{3,2,1,0:T(8,128)(2,1)S(1)} all-to-all(bf16[16,8,128,128]{3,2,1,0:T(8,128)(2,1)} %bitcast.116), channel_id=1, replica_groups={{0,8,16,24,32,40,48,56,64,72,80,88,96,104,112,120},{4,12,20,28,36,44,52..., dimensions={0} | all-to-all | bytes 8388608 | tf_op jit(solution)/shard_map/all_to_all | solution.py:442
  (189 shorter events, 149.2 us)
Async XLA Ops:
  6.5 354.4 %reduce-scatter.2.cloned.1.call-start = ((), (), s32[]{:S(2)}) async-start(), calls=%async_computation.2 | async-start | bytes 4456448 | tf_op jit(solution)/shard_map/reduce_scatter | solution.py:451
  21.2 10.0 %collective-permute-start = (bf16[33,32,128]{2,1,0:T(8,128)(2,1)S(1)}, bf16[33,32,128]{2,1,0:T(8,128)(2,1)S(1)}, u32[]{:S(2)}, u32[]{:S(2)}) collective-permute-start(bf16[33,32,128]{2,1,0:T(8,128)(2,1)S(1)} %get-tuple-element.117), channel_id=1, source_target_pairs={{0,1},{1,2},{2,3},{3,0},{4,5},{5,6},{6,7},{7,4},{8,9},{9,10},{10,1... | collective-permute-start | bytes 811016 | tf_op jit(solution)/shard_map/ppermute | solution.py:391
  35.6 8.9 %collective-permute-start.1 = (bf16[33,32,128]{2,1,0:T(8,128)(2,1)S(1)}, bf16[33,32,128]{2,1,0:T(8,128)(2,1)S(1)}, u32[]{:S(2)}, u32[]{:S(2)}) collective-permute-start(bf16[33,32,128]{2,1,0:T(8,128)(2,1)S(1)} %get-tuple-element.121.refs_7_), channel_id=1, source_target_pairs={{0,1},{1,2},{2,3},{3,0},{4,5},{5,6},{6,7},{7,4},{8,9},{9,10},{10,1... | collective-permute-start | bytes 811016 | tf_op jit(solution)/shard_map/ppermute | solution.py:391
  35.7 16.7 %collective-permute-start.3 = (bf16[2,32,32,128]{3,2,1,0:T(8,128)(2,1)S(1)}, bf16[2,32,32,128]{3,2,1,0:T(8,128)(2,1)S(1)}, u32[]{:S(2)}, u32[]{:S(2)}) collective-permute-start(bf16[2,32,32,128]{3,2,1,0:T(8,128)(2,1)S(1)} %get-tuple-element.129), channel_id=1, source_target_pairs={{0,3},{1,0},{2,1},{3,2},{4,7},{5,4},{6,5},{7,6},{8,11},{9,8},{10,9... | collective-permute-start | bytes 1572872 | tf_op jit(solution)/shard_map/ppermute | solution.py:391
  49.1 8.0 %collective-permute-start.2 = (bf16[33,32,128]{2,1,0:T(8,128)(2,1)S(1)}, bf16[33,32,128]{2,1,0:T(8,128)(2,1)S(1)}, u32[]{:S(2)}, u32[]{:S(2)}) collective-permute-start(bf16[33,32,128]{2,1,0:T(8,128)(2,1)S(1)} %get-tuple-element.128), channel_id=1, source_target_pairs={{0,1},{1,2},{2,3},{3,0},{4,5},{5,6},{6,7},{7,4},{8,9},{9,10},{10,1... | collective-permute-start | bytes 811016 | tf_op jit(solution)/shard_map/ppermute | solution.py:391
  49.1 12.7 %collective-permute-start.5 = (bf16[2,32,32,128]{3,2,1,0:T(8,128)(2,1)S(1)}, bf16[2,32,32,128]{3,2,1,0:T(8,128)(2,1)S(1)}, u32[]{:S(2)}, u32[]{:S(2)}) collective-permute-start(bf16[2,32,32,128]{3,2,1,0:T(8,128)(2,1)S(1)} %get-tuple-element.132), channel_id=1, source_target_pairs={{0,3},{1,0},{2,1},{3,2},{4,7},{5,4},{6,5},{7,6},{8,11},{9,8},{10,9... | collective-permute-start | bytes 1572872 | tf_op jit(solution)/shard_map/ppermute | solution.py:391
  74.7 12.9 %collective-permute-start.8 = (bf16[2,32,32,128]{3,2,1,0:T(8,128)(2,1)S(1)}, bf16[2,32,32,128]{3,2,1,0:T(8,128)(2,1)S(1)}, u32[]{:S(2)}, u32[]{:S(2)}) collective-permute-start(bf16[2,32,32,128]{3,2,1,0:T(8,128)(2,1)S(1)} %get-tuple-element.138), channel_id=1, source_target_pairs={{0,3},{1,0},{2,1},{3,2},{4,7},{5,4},{6,5},{7,6},{8,11},{9,8},{10,9... | collective-permute-start | bytes 1572872 | tf_op jit(solution)/shard_map/ppermute | solution.py:391
  87.5 7.7 %collective-permute-start.7 = (bf16[33,32,128]{2,1,0:T(8,128)(2,1)S(1)}, bf16[33,32,128]{2,1,0:T(8,128)(2,1)S(1)}, u32[]{:S(2)}, u32[]{:S(2)}) collective-permute-start(bf16[33,32,128]{2,1,0:T(8,128)(2,1)S(1)} %get-tuple-element.137.refs_9_), channel_id=1, source_target_pairs={{0,1},{1,2},{2,3},{3,0},{4,5},{5,6},{6,7},{7,4},{8,9},{9,10},{10,1... | collective-permute-start | bytes 811016 | tf_op jit(solution)/shard_map/ppermute | solution.py:391
  100.5 12.9 %collective-permute-start.12 = (bf16[2,32,32,128]{3,2,1,0:T(8,128)(2,1)S(1)}, bf16[2,32,32,128]{3,2,1,0:T(8,128)(2,1)S(1)}, u32[]{:S(2)}, u32[]{:S(2)}) collective-permute-start(bf16[2,32,32,128]{3,2,1,0:T(8,128)(2,1)S(1)} %get-tuple-element.149), channel_id=1, source_target_pairs={{0,3},{1,0},{2,1},{3,2},{4,7},{5,4},{6,5},{7,6},{8,11},{9,8},{10,9... | collective-permute-start | bytes 1572872 | tf_op jit(solution)/shard_map/ppermute | solution.py:391
  126.3 8.3 %collective-permute-start.13 = (bf16[33,32,128]{2,1,0:T(8,128)(2,1)S(1)}, bf16[33,32,128]{2,1,0:T(8,128)(2,1)S(1)}, u32[]{:S(2)}, u32[]{:S(2)}) collective-permute-start(bf16[33,32,128]{2,1,0:T(8,128)(2,1)S(1)} %get-tuple-element.153), channel_id=1, source_target_pairs={{0,1},{1,2},{2,3},{3,0},{4,5},{5,6},{6,7},{7,4},{8,9},{9,10},{10,1... | collective-permute-start | bytes 811016 | tf_op jit(solution)/shard_map/ppermute | solution.py:391
  126.4 13.3 %collective-permute-start.15 = (bf16[2,32,32,128]{3,2,1,0:T(8,128)(2,1)S(1)}, bf16[2,32,32,128]{3,2,1,0:T(8,128)(2,1)S(1)}, u32[]{:S(2)}, u32[]{:S(2)}) collective-permute-start(bf16[2,32,32,128]{3,2,1,0:T(8,128)(2,1)S(1)} %get-tuple-element.158), channel_id=1, source_target_pairs={{0,3},{1,0},{2,1},{3,2},{4,7},{5,4},{6,5},{7,6},{8,11},{9,8},{10,9... | collective-permute-start | bytes 1572872 | tf_op jit(solution)/shard_map/ppermute | solution.py:391
  156.8 8.5 %collective-permute-start.16 = (bf16[33,32,128]{2,1,0:T(8,128)(2,1)S(1)}, bf16[33,32,128]{2,1,0:T(8,128)(2,1)S(1)}, u32[]{:S(2)}, u32[]{:S(2)}) collective-permute-start(bf16[33,32,128]{2,1,0:T(8,128)(2,1)S(1)} %get-tuple-element.177), channel_id=1, source_target_pairs={{0,3},{1,0},{2,1},{3,2},{4,7},{5,4},{6,5},{7,6},{8,11},{9,8},{10,9... | collective-permute-start | bytes 811016 | tf_op jit(solution)/shard_map/ppermute | solution.py:391
  166.0 12.4 %collective-permute-start.17 = (bf16[33,32,128]{2,1,0:T(8,128)(2,1)S(1)}, bf16[33,32,128]{2,1,0:T(8,128)(2,1)S(1)}, u32[]{:S(2)}, u32[]{:S(2)}) collective-permute-start(bf16[33,32,128]{2,1,0:T(8,128)(2,1)S(1)} %get-tuple-element.179.refs_10_), channel_id=1, source_target_pairs={{0,3},{1,0},{2,1},{3,2},{4,7},{5,4},{6,5},{7,6},{8,11},{9,8},{10,9... | collective-permute-start | bytes 811016 | tf_op jit(solution)/shard_map/ppermute | solution.py:391
  173.0 14.3 %collective-permute-start.19 = (bf16[2,32,32,128]{3,2,1,0:T(8,128)(2,1)S(1)}, bf16[2,32,32,128]{3,2,1,0:T(8,128)(2,1)S(1)}, u32[]{:S(2)}, u32[]{:S(2)}) collective-permute-start(bf16[2,32,32,128]{3,2,1,0:T(8,128)(2,1)S(1)} %get-tuple-element.192), channel_id=1, source_target_pairs={{0,1},{1,2},{2,3},{3,0},{4,5},{5,6},{6,7},{7,4},{8,9},{9,10},{10,1... | collective-permute-start | bytes 1572872 | tf_op jit(solution)/shard_map/ppermute | solution.py:391
  179.3 11.4 %collective-permute-start.18 = (bf16[33,32,128]{2,1,0:T(8,128)(2,1)S(1)}, bf16[33,32,128]{2,1,0:T(8,128)(2,1)S(1)}, u32[]{:S(2)}, u32[]{:S(2)}) collective-permute-start(bf16[33,32,128]{2,1,0:T(8,128)(2,1)S(1)} %get-tuple-element.191), channel_id=1, source_target_pairs={{0,3},{1,0},{2,1},{3,2},{4,7},{5,4},{6,5},{7,6},{8,11},{9,8},{10,9... | collective-permute-start | bytes 811016 | tf_op jit(solution)/shard_map/ppermute | solution.py:391
  186.2 12.2 %collective-permute-start.21 = (bf16[2,32,32,128]{3,2,1,0:T(8,128)(2,1)S(1)}, bf16[2,32,32,128]{3,2,1,0:T(8,128)(2,1)S(1)}, u32[]{:S(2)}, u32[]{:S(2)}) collective-permute-start(bf16[2,32,32,128]{3,2,1,0:T(8,128)(2,1)S(1)} %get-tuple-element.195), channel_id=1, source_target_pairs={{0,1},{1,2},{2,3},{3,0},{4,5},{5,6},{6,7},{7,4},{8,9},{9,10},{10,1... | collective-permute-start | bytes 1572872 | tf_op jit(solution)/shard_map/ppermute | solution.py:391
  209.1 10.6 %collective-permute-start.24 = (bf16[2,32,32,128]{3,2,1,0:T(8,128)(2,1)S(1)}, bf16[2,32,32,128]{3,2,1,0:T(8,128)(2,1)S(1)}, u32[]{:S(2)}, u32[]{:S(2)}) collective-permute-start(bf16[2,32,32,128]{3,2,1,0:T(8,128)(2,1)S(1)} %get-tuple-element.201), channel_id=1, source_target_pairs={{0,1},{1,2},{2,3},{3,0},{4,5},{5,6},{6,7},{7,4},{8,9},{9,10},{10,1... | collective-permute-start | bytes 1572872 | tf_op jit(solution)/shard_map/ppermute | solution.py:391
  219.7 11.6 %collective-permute-start.25 = (bf16[4,32,32,128]{3,2,1,0:T(8,128)(2,1)S(1)}, bf16[4,32,32,128]{3,2,1,0:T(8,128)(2,1)S(1)}, u32[]{:S(2)}, u32[]{:S(2)}) collective-permute-start(bf16[4,32,32,128]{3,2,1,0:T(8,128)(2,1)S(1)} %copy-done.5), channel_id=1, source_target_pairs={{0,4},{4,0},{8,12},{12,8},{16,20},{20,16},{24,28},{28,24},{32,36},... | collective-permute-start | bytes 3145736 | tf_op jit(solution)/shard_map/ppermute | solution.py:435
  231.1 10.9 %collective-permute-start.27 = (bf16[33,32,128]{2,1,0:T(8,128)(2,1)}, bf16[33,32,128]{2,1,0:T(8,128)(2,1)S(1)}, u32[]{:S(2)}, u32[]{:S(2)}) collective-permute-start(bf16[33,32,128]{2,1,0:T(8,128)(2,1)} %get-tuple-element.216), channel_id=1, source_target_pairs={{0,3},{1,0},{2,1},{3,2},{4,7},{5,4},{6,5},{7,6},{8,11},{9,8},{10,9... | collective-permute-start | bytes 811016 | tf_op jit(solution)/shard_map/ppermute | solution.py:391
  242.0 15.2 %collective-permute-start.29 = (bf16[2,32,32,128]{3,2,1,0:T(8,128)(2,1)S(1)}, bf16[2,32,32,128]{3,2,1,0:T(8,128)(2,1)S(1)}, u32[]{:S(2)}, u32[]{:S(2)}) collective-permute-start(bf16[2,32,32,128]{3,2,1,0:T(8,128)(2,1)S(1)} %get-tuple-element.220), channel_id=1, source_target_pairs={{0,1},{1,2},{2,3},{3,0},{4,5},{5,6},{6,7},{7,4},{8,9},{9,10},{10,1... | collective-permute-start | bytes 1572872 | tf_op jit(solution)/shard_map/ppermute | solution.py:391
  249.5 8.6 %collective-permute-start.28 = (bf16[33,32,128]{2,1,0:T(8,128)(2,1)S(1)}, bf16[33,32,128]{2,1,0:T(8,128)(2,1)S(1)}, u32[]{:S(2)}, u32[]{:S(2)}) collective-permute-start(bf16[33,32,128]{2,1,0:T(8,128)(2,1)S(1)} %get-tuple-element.219.refs_11_), channel_id=1, source_target_pairs={{0,3},{1,0},{2,1},{3,2},{4,7},{5,4},{6,5},{7,6},{8,11},{9,8},{10,9... | collective-permute-start | bytes 811016 | tf_op jit(solution)/shard_map/ppermute | solution.py:391
  262.1 7.7 %collective-permute-start.30 = (bf16[33,32,128]{2,1,0:T(8,128)(2,1)S(1)}, bf16[33,32,128]{2,1,0:T(8,128)(2,1)S(1)}, u32[]{:S(2)}, u32[]{:S(2)}) collective-permute-start(bf16[33,32,128]{2,1,0:T(8,128)(2,1)S(1)} %get-tuple-element.222), channel_id=1, source_target_pairs={{0,3},{1,0},{2,1},{3,2},{4,7},{5,4},{6,5},{7,6},{8,11},{9,8},{10,9... | collective-permute-start | bytes 811016 | tf_op jit(solution)/shard_map/ppermute | solution.py:391
  262.2 14.4 %collective-permute-start.32 = (bf16[2,32,32,128]{3,2,1,0:T(8,128)(2,1)S(1)}, bf16[2,32,32,128]{3,2,1,0:T(8,128)(2,1)S(1)}, u32[]{:S(2)}, u32[]{:S(2)}) collective-permute-start(bf16[2,32,32,128]{3,2,1,0:T(8,128)(2,1)S(1)} %get-tuple-element.225), channel_id=1, source_target_pairs={{0,1},{1,2},{2,3},{3,0},{4,5},{5,6},{6,7},{7,4},{8,9},{9,10},{10,1... | collective-permute-start | bytes 1572872 | tf_op jit(solution)/shard_map/ppermute | solution.py:391
  273.9 11.6 %collective-permute-start.9 = (bf16[4,32,32,128]{3,2,1,0:T(8,128)(2,1)S(1)}, bf16[4,32,32,128]{3,2,1,0:T(8,128)(2,1)S(1)}, u32[]{:S(2)}, u32[]{:S(2)}) collective-permute-start(bf16[4,32,32,128]{3,2,1,0:T(8,128)(2,1)S(1)} %copy-done.6), channel_id=1, source_target_pairs={{0,4},{4,0},{8,12},{12,8},{16,20},{20,16},{24,28},{28,24},{32,36},... | collective-permute-start | bytes 3145736 | tf_op jit(solution)/shard_map/ppermute | solution.py:435
  (67 other events, 881.5 us)
Sparse Core Ops, SparseCore 0:
  242.1 105.4 reduce-scatter.1

commit v2 on v1

--- a/solution.py
+++ b/solution.py
@@ -27,12 +27,12 @@
     return jnp.where(lane == 0, high, jnp.where(lane == 1, low, 0.0)).astype(bf16)
 
 
-def tile_loop(gather_from, scatter_to, first, live, trash, source, weights, offset, acc):
+def tile_loop(table, gather_at, scatter_at, live, trash, source, weights, offset, acc):
     def group(g, carry):
         for k in range(UNROLL):
             n = g * UNROLL + k
-            put = jnp.where(n < live, scatter_to[first + n], trash)
-            acc[put] += jnp.dot(source[gather_from[first + n]], weights[offset + n], preferred_element_type=f32)
+            put = jnp.where(n < live, table[scatter_at + n], trash)
+            acc[put] += jnp.dot(source[table[gather_at + n]], weights[offset + n], preferred_element_type=f32)
         return carry
 
     lax.fori_loop(0, (live + UNROLL - 1) // UNROLL, group, 0)
@@ -57,6 +57,8 @@
         self.bundle = 2 * LAG
         self.ticks = turns * self.units + self.span
         self.section, self.half = turns, turns + 1
+        self.rows_at = turns + 2
+        self.cols_at = self.rows_at + turns * slots
 
     def piece(self, dtype, extra=0):
         return jax.ShapeDtypeStruct((self.grid + extra, self.rows, self.tile), dtype)
@@ -156,13 +158,15 @@
 
         def multiply(turn):
             live = tab[turn]
-            gather_from, scatter_to = (ref["rows"], ref["cols"]) if forward else (ref["cols"], ref["rows"])
+            gather_at, scatter_at = (plan.rows_at, plan.cols_at) if forward else (plan.cols_at, plan.rows_at)
             if forward:
-                tile_loop(gather_from, scatter_to, turn * plan.slots, live, G, source, ref["weights"], turn * plan.slots, acc)
+                first = turn * plan.slots
+                tile_loop(tab, gather_at + first, scatter_at + first, live, G, source, ref["weights"], first, acc)
             for place in turns_here * (not forward):
                 @pl.when(turn == place)
                 def _():
-                    tile_loop(gather_from, scatter_to, place * plan.slots, live, G, source, ref["weights%d" % place], 0, acc)
+                    first = place * plan.slots
+                    tile_loop(tab, gather_at + first, scatter_at + first, live, G, source, ref["weights%d" % place], 0, acc)
 
         @pl.when(active)
         def _():
@@ -268,19 +272,22 @@
                 out["bundle"][plan.bundle - 1] = jnp.zeros((G, T, B), bf16)
             if turning:
                 flipped = own["flipped"]
-                moves = []
-                for place in range(2):
-
-                    def flip(i, carry):
-                        for k in range(FLIP):
-                            at = i * FLIP + k
-                            flipped[place, at] = ref["weights"][place * plan.slots + piece * share + at].T
-                        return carry
-
-                    lax.fori_loop(0, piece_size // FLIP, flip, 0)
-                    moves.append(pltpu.make_async_copy(
-                        flipped.at[place], out["turned%d" % place].at[pl.ds(piece * share, piece_size)], sems.at[place]))
-                    moves[-1].start()
+
+                rounds = piece_size // FLIP
+
+                def flip(i, carry):
+                    place = i // rounds
+                    for k in range(FLIP):
+                        at = (i - place * rounds) * FLIP + k
+                        flipped[place, at] = ref["weights"][place * plan.slots + piece * share + at].T
+                    return carry
+
+                lax.fori_loop(0, 2 * rounds, flip, 0)
+                moves = [pltpu.make_async_copy(
+                    flipped.at[place], out["turned%d" % place].at[pl.ds(piece * share, piece_size)], sems.at[place])
+                    for place in range(2)]
+                for copy in moves:
+                    copy.start()
                 for copy in moves:
                     copy.wait()
 
@@ -290,7 +297,7 @@
     ins = list(named.values()) + list(pack) + list(alias_from.values())
     outs = pl.pallas_call(
         kernel,
-        in_specs=[SM] * 3 + [VM] * (len(names) - 3 + len(pack)) + [HBM] * len(alias_from),
+        in_specs=[SM] + [VM] * (len(names) - 1 + len(pack)) + [HBM] * len(alias_from),
         out_specs=[spec for spec, _ in shapes.values()],
         out_shape=[shape for _, shape in shapes.values()],
         input_output_aliases={len(names) + len(pack) + i: out_names.index(name) for i, name in enumerate(alias_from)},
@@ -301,14 +308,14 @@
     return dict(zip(out_names, outs))
 
 
-def tile_grads(plan, turn, info, rows, cols, normed_parts, error_parts, share, parts):
+def tile_grads(plan, turn, info, normed_parts, error_parts, share, parts):
     G, T, B, M = plan.grid, plan.rows, plan.tile, plan.units
     local = plan.slots // parts
     steps = 8
     chunk = local // steps
     tokens = M * T
 
-    def kernel(tab, rows_at, cols_at, *refs):
+    def kernel(tab, *refs):
         normeds, errors = refs[:parts], refs[parts:2 * parts]
         out, turned, flat = refs[-3:]
         step = pl.program_id(0)
@@ -329,14 +336,14 @@
             i = step * chunk + k
             n = (i // share) * (share * parts) + half * share + i % share
             at = turn * plan.slots + n
-            made = jnp.dot(turned[rows_at[at]], flat[cols_at[at]], preferred_element_type=f32)
+            made = jnp.dot(turned[tab[plan.rows_at + at]], flat[tab[plan.cols_at + at]], preferred_element_type=f32)
             out[k] = jnp.where(n < live, made, 0.0).astype(bf16)
 
     whole = pl.BlockSpec((M, G, T, B), lambda i, *_: (0, 0, 0, 0))
     return pl.pallas_call(
         kernel,
         grid_spec=pltpu.PrefetchScalarGridSpec(
-            num_scalar_prefetch=3,
+            num_scalar_prefetch=1,
             grid=(steps,),
             in_specs=[whole] * (2 * parts),
             out_specs=pl.BlockSpec((chunk, B, B), lambda i, *_: (i, 0, 0)),
@@ -346,7 +353,7 @@
         compiler_params=pltpu.CompilerParams(vmem_limit_bytes=GRAD_LIMIT),
         cost_estimate=pl.CostEstimate(flops=2 * local * B * B * parts * tokens, transcendentals=0, bytes_accessed=24 * 2**20),
         name="tile_grads",
-    )(info, rows, cols, *normed_parts, *error_parts)
+    )(info, *normed_parts, *error_parts)
 
 
 def sum_parts(parts):
@@ -380,8 +387,9 @@
     plan = Plan(sections, turns, slots, tile, grid, tokens)
     M, T = plan.units, plan.rows
 
-    rows, cols = block_rows.reshape(-1), block_cols.reshape(-1)
-    info = jnp.concatenate([block_counts.reshape(-1), section_pos[None], core[None]])
+    info = jnp.concatenate(
+        [block_counts.reshape(-1), section_pos[None], core[None], block_rows.reshape(-1), block_cols.reshape(-1)]
+    )
     entering = hidden_in.reshape(M, T, 2 * half_width)
     entering_grad = out_grad.reshape(M, T, 2 * half_width)
     weights = blocks.reshape(turns * slots, tile, tile)
@@ -397,7 +405,7 @@
         for order in range(plan.ticks):
             tick = order if forward else plan.ticks - 1 - order
             use_entering, use_prev = order < M + plan.span, order >= M
-            named = dict(info=info, rows=rows, cols=cols, gains=gain_rows)
+            named = dict(info=info, gains=gain_rows)
             if forward:
                 named["weights"] = weights
             else:
@@ -436,7 +444,7 @@
 
     def make_grads(turn, stores):
         name = "store%d" % turn
-        return tile_grads(plan, turn, info, rows, cols, gather(normed[name]), gather(stores[name]), share, PARTS)
+        return tile_grads(plan, turn, info, gather(normed[name]), gather(stores[name]), share, PARTS)
 
     def trade(part):
         return lax.all_to_all(

time: 369 us -> 362 us (0.981); the launches traced: 370 us -> 356 us
  Pallas kernels: 107 us -> 93.6 us
    pallas_call x22, Pallas kernels: 92.7 us -> 79.1 us  [tick_call(): pl.pallas_call(kernel, in_specs=[SM] + [VM] * (len(names) - 1 + len(pack)...]
    unnamed x112 -> x104, local copies, waits for them, and re-layouts: 18.9 us -> 17.5 us
  transfers between devices with their start and end apart: 35 -> 35, of which waited for: 25 -> 26; matrix products, arithmetic and copies ran while one was open for 0% -> 0% of each run, Pallas kernels for 19% -> 17%
where the time goes in v2:
time: 362 us; the launch traced here: 356 us
  waiting for transfers between devices  118 us (33%)
  Pallas kernels  93.6 us (26%)
  blocking collectives  63.5 us (18%)
  starting transfers between devices  46.9 us (13%)
  local copies, waits for them, and re-layouts  18.3 us (5%)
  between operations  14.1 us (4%)
    ppermute x30, waiting for transfers between devices, ring(): lax.ppermute(part, 'section', [(i, (i + by) % sections) for i in range(se...  112 us
    pallas_call x22, Pallas kernels, tick_call(): pl.pallas_call(kernel, in_specs=[SM] + [VM] * (len(names) - 1 + len(pack)...  79.1 us
    all_to_all x1, blocking collectives, trade(): lax.all_to_all(part.reshape(members, share, tile, tile), 'dp', 0, 0, axis...  63.5 us
    ppermute x30, starting transfers between devices, ring(): lax.ppermute(part, 'section', [(i, (i + by) % sections) for i in range(se...  46.6 us
    unnamed x104, local copies, waits for them, and re-layouts  17.5 us
    pallas_call x2, Pallas kernels, tile_grads(): pl.pallas_call(kernel, grid_spec=pltpu.PrefetchScalarGridSpec(num_scalar_...  13.6 us
  transfers between devices with their start and end apart: 35, of which 26 were waited for; matrix products, arithmetic and copies ran while one was open for 0% of the time, Pallas kernels for 17%

profile of v2, /device:TPU:0, one launch (start us, length us, event | category | flops | bytes accessed | tf_op | source)
XLA Modules:
  0.0 355.9 jit_solution(8846022911692801211)
XLA Ops:
  7.3 5.8 %copy-done = bf16[2,1,256,128,128]{4,3,2,1,0:T(8,128)(2,1)S(1)} copy-done((bf16[2,1,256,128,128]{4,3,2,1,0:T(8,128)(2,1)S(1)}, bf16[2,1,256,128,128]{4,3,2,1,0:T(8,128)(2,1)}, u32[]{:S(2)}) %copy-start) | copy-done | bytes 16777240
  23.2 7.7 %collective-permute-done.refs_4_ = bf16[33,32,128]{2,1,0:T(8,128)(2,1)S(1)} collective-permute-done((bf16[33,32,128]{2,1,0:T(8,128)(2,1)S(1)}, bf16[33,32,128]{2,1,0:T(8,128)(2,1)S(1)}, u32[]{:S(2)}, u32[]{:S(2)}) %collective-permute-start) | collective-permute-done | bytes 270368 | tf_op jit(solution)/shard_map/ppermute | solution.py:399
  39.0 5.5 %collective-permute-done.1.refs_4_ = bf16[33,32,128]{2,1,0:T(8,128)(2,1)S(1)} collective-permute-done((bf16[33,32,128]{2,1,0:T(8,128)(2,1)S(1)}, bf16[33,32,128]{2,1,0:T(8,128)(2,1)S(1)}, u32[]{:S(2)}, u32[]{:S(2)}) %collective-permute-start.1) | collective-permute-done | bytes 270368 | tf_op jit(solution)/shard_map/ppermute | solution.py:399
  52.1 4.6 %collective-permute-done.2.refs_4_ = bf16[33,32,128]{2,1,0:T(8,128)(2,1)S(1)} collective-permute-done((bf16[33,32,128]{2,1,0:T(8,128)(2,1)S(1)}, bf16[33,32,128]{2,1,0:T(8,128)(2,1)S(1)}, u32[]{:S(2)}, u32[]{:S(2)}) %collective-permute-start.2) | collective-permute-done | bytes 270368 | tf_op jit(solution)/shard_map/ppermute | solution.py:399
  61.5 6.6 %collective-permute-done.4.refs_5_ = bf16[33,32,128]{2,1,0:T(8,128)(2,1)S(1)} collective-permute-done((bf16[33,32,128]{2,1,0:T(8,128)(2,1)S(1)}, bf16[33,32,128]{2,1,0:T(8,128)(2,1)S(1)}, u32[]{:S(2)}, u32[]{:S(2)}) %collective-permute-start.4) | collective-permute-done | bytes 270368 | tf_op jit(solution)/shard_map/ppermute | solution.py:399
  75.4 4.4 %collective-permute-done.6.refs_5_ = bf16[33,32,128]{2,1,0:T(8,128)(2,1)S(1)} collective-permute-done((bf16[33,32,128]{2,1,0:T(8,128)(2,1)S(1)}, bf16[33,32,128]{2,1,0:T(8,128)(2,1)S(1)}, u32[]{:S(2)}, u32[]{:S(2)}) %collective-permute-start.6) | collective-permute-done | bytes 270368 | tf_op jit(solution)/shard_map/ppermute | solution.py:399
  83.9 7.6 %collective-permute-done.7.refs_5_ = bf16[33,32,128]{2,1,0:T(8,128)(2,1)S(1)} collective-permute-done((bf16[33,32,128]{2,1,0:T(8,128)(2,1)S(1)}, bf16[33,32,128]{2,1,0:T(8,128)(2,1)S(1)}, u32[]{:S(2)}, u32[]{:S(2)}) %collective-permute-start.7) | collective-permute-done | bytes 270368 | tf_op jit(solution)/shard_map/ppermute | solution.py:399
  98.8 4.4 %collective-permute-done.10.refs_4_ = bf16[33,32,128]{2,1,0:T(8,128)(2,1)S(1)} collective-permute-done((bf16[33,32,128]{2,1,0:T(8,128)(2,1)S(1)}, bf16[33,32,128]{2,1,0:T(8,128)(2,1)S(1)}, u32[]{:S(2)}, u32[]{:S(2)}) %collective-permute-start.10) | collective-permute-done | bytes 270368 | tf_op jit(solution)/shard_map/ppermute | solution.py:399
  107.2 7.6 %collective-permute-done.11.refs_4_ = bf16[33,32,128]{2,1,0:T(8,128)(2,1)S(1)} collective-permute-done((bf16[33,32,128]{2,1,0:T(8,128)(2,1)S(1)}, bf16[33,32,128]{2,1,0:T(8,128)(2,1)S(1)}, u32[]{:S(2)}, u32[]{:S(2)}) %collective-permute-start.11) | collective-permute-done | bytes 270368 | tf_op jit(solution)/shard_map/ppermute | solution.py:399
  114.8 6.2 %forward_tick.19 = (bf16[33,32,128]{2,1,0:T(8,128)(2,1)S(1)}, bf16[32,32,128]{2,1,0:T(8,128)(2,1)}, bf16[32,32,128]{2,1,0:T(8,128)(2,1)}, f32[32,128]{1,0:T(8,12...) custom-call(s32[1028]{0:T(1024)S(1)} %concatenate.3.refs_0_.tab, ...), custom_call_target="tpu_custom_call", output_to_operand_aliasing={{4}: (7, {}), {5}: (8, {}), {6}: (9, {})} | custom-call | tf_op jit(solution)/shard_map/forward_tick/pallas_call | solution.py:298
  124.5 4.4 %collective-permute-done.13.refs_4_ = bf16[33,32,128]{2,1,0:T(8,128)(2,1)S(1)} collective-permute-done((bf16[33,32,128]{2,1,0:T(8,128)(2,1)S(1)}, bf16[33,32,128]{2,1,0:T(8,128)(2,1)S(1)}, u32[]{:S(2)}, u32[]{:S(2)}) %collective-permute-start.13) | collective-permute-done | bytes 270368 | tf_op jit(solution)/shard_map/ppermute | solution.py:399
  128.9 6.1 %forward_tick.20 = (bf16[33,32,128]{2,1,0:T(8,128)(2,1)S(1)}, bf16[32,32,128]{2,1,0:T(8,128)(2,1)}, bf16[32,32,128]{2,1,0:T(8,128)(2,1)}, f32[32,128]{1,0:T(8,12...) custom-call(s32[1028]{0:T(1024)S(1)} %concatenate.3.refs_0_.tab, ...), custom_call_target="tpu_custom_call", output_to_operand_aliasing={{4}: (6, {}), {5}: (7, {}), {6}: (8, {})} | custom-call | tf_op jit(solution)/shard_map/forward_tick/pallas_call | solution.py:298
  135.1 7.6 %collective-permute-done.14.refs_4_ = bf16[33,32,128]{2,1,0:T(8,128)(2,1)S(1)} collective-permute-done((bf16[33,32,128]{2,1,0:T(8,128)(2,1)S(1)}, bf16[33,32,128]{2,1,0:T(8,128)(2,1)S(1)}, u32[]{:S(2)}, u32[]{:S(2)}) %collective-permute-start.14) | collective-permute-done | bytes 270368 | tf_op jit(solution)/shard_map/ppermute | solution.py:399
  142.8 6.4 %forward_tick.21 = (bf16[33,32,128]{2,1,0:T(8,128)(2,1)}, bf16[32,32,128]{2,1,0:T(8,128)(2,1)S(1)}, bf16[32,32,128]{2,1,0:T(8,128)(2,1)S(1)}, f32[32,128]{1,0:T(...) custom-call(s32[1028]{0:T(1024)S(1)} %concatenate.3.refs_0_.tab, ...), custom_call_target="tpu_custom_call", output_to_operand_aliasing={{4}: (6, {}), {5}: (7, {}), {6}: (8, {})} | custom-call | tf_op jit(solution)/shard_map/forward_tick/pallas_call | solution.py:298
  153.4 6.4 %collective-permute-done.16.refs_7_ = bf16[33,32,128]{2,1,0:T(8,128)(2,1)S(1)} collective-permute-done((bf16[33,32,128]{2,1,0:T(8,128)(2,1)S(1)}, bf16[33,32,128]{2,1,0:T(8,128)(2,1)S(1)}, u32[]{:S(2)}, u32[]{:S(2)}) %collective-permute-start.16) | collective-permute-done | bytes 270368 | tf_op jit(solution)/shard_map/ppermute | solution.py:399
  160.6 4.9 %collective-permute-start.17 = (bf16[33,32,128]{2,1,0:T(8,128)(2,1)S(1)}, bf16[33,32,128]{2,1,0:T(8,128)(2,1)S(1)}, u32[]{:S(2)}, u32[]{:S(2)}) collective-permute-start(bf16[33,32,128]{2,1,0:T(8,128)(2,1)S(1)} %get-tuple-element.179.refs_8_), channel_id=1, source_target_pairs={{0,3},{1,0},{2,1},{3,2},{4,7},{5,4},{6,5},{7,6},{8,11},{9,8},{10,9... | collective-permute-start | bytes 811016 | tf_op jit(solution)/shard_map/ppermute | solution.py:399
  165.5 4.4 %collective-permute-done.17.refs_7_ = bf16[33,32,128]{2,1,0:T(8,128)(2,1)S(1)} collective-permute-done((bf16[33,32,128]{2,1,0:T(8,128)(2,1)S(1)}, bf16[33,32,128]{2,1,0:T(8,128)(2,1)S(1)}, u32[]{:S(2)}, u32[]{:S(2)}) %collective-permute-start.17) | collective-permute-done | bytes 270368 | tf_op jit(solution)/shard_map/ppermute | solution.py:399
  170.7 6.1 %collective-permute-start.18 = (bf16[33,32,128]{2,1,0:T(8,128)(2,1)S(1)}, bf16[33,32,128]{2,1,0:T(8,128)(2,1)S(1)}, u32[]{:S(2)}, u32[]{:S(2)}) collective-permute-start(bf16[33,32,128]{2,1,0:T(8,128)(2,1)S(1)} %get-tuple-element.191), channel_id=1, source_target_pairs={{0,3},{1,0},{2,1},{3,2},{4,7},{5,4},{6,5},{7,6},{8,11},{9,8},{10,9... | collective-permute-start | bytes 811016 | tf_op jit(solution)/shard_map/ppermute | solution.py:399
  208.3 6.3 %collective-permute-done.23.refs_9_ = bf16[33,32,128]{2,1,0:T(8,128)(2,1)S(1)} collective-permute-done((bf16[33,32,128]{2,1,0:T(8,128)(2,1)S(1)}, bf16[33,32,128]{2,1,0:T(8,128)(2,1)S(1)}, u32[]{:S(2)}, u32[]{:S(2)}) %collective-permute-start.23) | collective-permute-done | bytes 270368 | tf_op jit(solution)/shard_map/ppermute | solution.py:399
  223.2 6.8 %tile_grads.2 = bf16[128,128,128]{2,1,0:T(8,128)(2,1)} custom-call(s32[1028]{0:T(1024)S(1)} %concatenate.3.refs_0_.tab, bf16[4,32,32,128]{3,2,1,0:T(8,128)(2,1)S(1)} %copy-done.6, bf16[4,32,32,128]{3,2,1,0:T(8,128)(2,1)S(1)} %collective-permute-done.25.refs_1_, bf16[4,32,32,128]{3,2,1,0:T(8,128)(2,1)S(1)} %copy-done.7, ...), custom_call_target="tpu_custom_call" | custom-call | flops 1073741824 | bytes 25165824 | tf_op jit(solution)/shard_map/tile_grads/pallas_call | solution.py:343
  239.1 6.1 %collective-permute-done.29.refs_8_ = bf16[2,32,32,128]{3,2,1,0:T(8,128)(2,1)S(1)} collective-permute-done((bf16[2,32,32,128]{3,2,1,0:T(8,128)(2,1)S(1)}, bf16[2,32,32,128]{3,2,1,0:T(8,128)(2,1)S(1)}, u32[]{:S(2)}, u32[]{:S(2)}) %collective-permute-start.29) | collective-permute-done | bytes 524320 | tf_op jit(solution)/shard_map/ppermute | solution.py:399
  252.3 5.4 %collective-permute-done.30.refs_7_ = bf16[33,32,128]{2,1,0:T(8,128)(2,1)S(1)} collective-permute-done((bf16[33,32,128]{2,1,0:T(8,128)(2,1)S(1)}, bf16[33,32,128]{2,1,0:T(8,128)(2,1)S(1)}, u32[]{:S(2)}, u32[]{:S(2)}) %collective-permute-start.30) | collective-permute-done | bytes 270368 | tf_op jit(solution)/shard_map/ppermute | solution.py:399
  276.0 6.8 %tile_grads.3 = bf16[128,128,128]{2,1,0:T(8,128)(2,1)} custom-call(s32[1028]{0:T(1024)S(1)} %concatenate.3.refs_0_.tab, bf16[4,32,32,128]{3,2,1,0:T(8,128)(2,1)S(1)} %copy-done.5, bf16[4,32,32,128]{3,2,1,0:T(8,128)(2,1)S(1)} %collective-permute-done.9.refs_1_, bf16[4,32,32,128]{3,2,1,0:T(8,128)(2,1)S(1)} %copy-done.8, ...), custom_call_target="tpu_custom_call" | custom-call | flops 1073741824 | bytes 25165824 | tf_op jit(solution)/shard_map/tile_grads/pallas_call | solution.py:343
  282.7 63.5 %all_to_all.5.given = bf16[16,8,128,128]{3,2,1,0:T(8,128)(2,1)S(1)} all-to-all(bf16[16,8,128,128]{3,2,1,0:T(8,128)(2,1)} %bitcast.68), channel_id=1, replica_groups={{0,8,16,24,32,40,48,56,64,72,80,88,96,104,112,120},{4,12,20,28,36,44,52..., dimensions={0} | all-to-all | bytes 8388608 | tf_op jit(solution)/shard_map/all_to_all | solution.py:450
  (181 shorter events, 139.9 us)
Async XLA Ops:
  6.5 340.7 %reduce-scatter.2.cloned.1.call-start = ((), (), s32[]{:S(2)}) async-start(), calls=%async_computation.2 | async-start | bytes 4456448 | tf_op jit(solution)/shard_map/reduce_scatter | solution.py:459
  19.1 11.9 %collective-permute-start = (bf16[33,32,128]{2,1,0:T(8,128)(2,1)S(1)}, bf16[33,32,128]{2,1,0:T(8,128)(2,1)S(1)}, u32[]{:S(2)}, u32[]{:S(2)}) collective-permute-start(bf16[33,32,128]{2,1,0:T(8,128)(2,1)S(1)} %get-tuple-element.117), channel_id=1, source_target_pairs={{0,1},{1,2},{2,3},{3,0},{4,5},{5,6},{6,7},{7,4},{8,9},{9,10},{10,1... | collective-permute-start | bytes 811016 | tf_op jit(solution)/shard_map/ppermute | solution.py:399
  34.6 9.9 %collective-permute-start.1 = (bf16[33,32,128]{2,1,0:T(8,128)(2,1)S(1)}, bf16[33,32,128]{2,1,0:T(8,128)(2,1)S(1)}, u32[]{:S(2)}, u32[]{:S(2)}) collective-permute-start(bf16[33,32,128]{2,1,0:T(8,128)(2,1)S(1)} %get-tuple-element.121.refs_5_), channel_id=1, source_target_pairs={{0,1},{1,2},{2,3},{3,0},{4,5},{5,6},{6,7},{7,4},{8,9},{9,10},{10,1... | collective-permute-start | bytes 811016 | tf_op jit(solution)/shard_map/ppermute | solution.py:399
  35.4 16.7 %collective-permute-start.3 = (bf16[2,32,32,128]{3,2,1,0:T(8,128)(2,1)S(1)}, bf16[2,32,32,128]{3,2,1,0:T(8,128)(2,1)S(1)}, u32[]{:S(2)}, u32[]{:S(2)}) collective-permute-start(bf16[2,32,32,128]{3,2,1,0:T(8,128)(2,1)S(1)} %get-tuple-element.129), channel_id=1, source_target_pairs={{0,3},{1,0},{2,1},{3,2},{4,7},{5,4},{6,5},{7,6},{8,11},{9,8},{10,9... | collective-permute-start | bytes 1572872 | tf_op jit(solution)/shard_map/ppermute | solution.py:399
  48.2 8.6 %collective-permute-start.2 = (bf16[33,32,128]{2,1,0:T(8,128)(2,1)S(1)}, bf16[33,32,128]{2,1,0:T(8,128)(2,1)S(1)}, u32[]{:S(2)}, u32[]{:S(2)}) collective-permute-start(bf16[33,32,128]{2,1,0:T(8,128)(2,1)S(1)} %get-tuple-element.128), channel_id=1, source_target_pairs={{0,1},{1,2},{2,3},{3,0},{4,5},{5,6},{6,7},{7,4},{8,9},{9,10},{10,1... | collective-permute-start | bytes 811016 | tf_op jit(solution)/shard_map/ppermute | solution.py:399
  48.2 13.3 %collective-permute-start.5 = (bf16[2,32,32,128]{3,2,1,0:T(8,128)(2,1)S(1)}, bf16[2,32,32,128]{3,2,1,0:T(8,128)(2,1)S(1)}, u32[]{:S(2)}, u32[]{:S(2)}) collective-permute-start(bf16[2,32,32,128]{3,2,1,0:T(8,128)(2,1)S(1)} %get-tuple-element.132), channel_id=1, source_target_pairs={{0,3},{1,0},{2,1},{3,2},{4,7},{5,4},{6,5},{7,6},{8,11},{9,8},{10,9... | collective-permute-start | bytes 1572872 | tf_op jit(solution)/shard_map/ppermute | solution.py:399
  60.4 7.7 %collective-permute-start.4 = (bf16[33,32,128]{2,1,0:T(8,128)(2,1)S(1)}, bf16[33,32,128]{2,1,0:T(8,128)(2,1)S(1)}, u32[]{:S(2)}, u32[]{:S(2)}) collective-permute-start(bf16[33,32,128]{2,1,0:T(8,128)(2,1)S(1)} %get-tuple-element.131.refs_7_), channel_id=1, source_target_pairs={{0,1},{1,2},{2,3},{3,0},{4,5},{5,6},{6,7},{7,4},{8,9},{9,10},{10,1... | collective-permute-start | bytes 811016 | tf_op jit(solution)/shard_map/ppermute | solution.py:399
  72.1 7.7 %collective-permute-start.6 = (bf16[33,32,128]{2,1,0:T(8,128)(2,1)S(1)}, bf16[33,32,128]{2,1,0:T(8,128)(2,1)S(1)}, u32[]{:S(2)}, u32[]{:S(2)}) collective-permute-start(bf16[33,32,128]{2,1,0:T(8,128)(2,1)S(1)} %get-tuple-element.134), channel_id=1, source_target_pairs={{0,1},{1,2},{2,3},{3,0},{4,5},{5,6},{6,7},{7,4},{8,9},{9,10},{10,1... | collective-permute-start | bytes 811016 | tf_op jit(solution)/shard_map/ppermute | solution.py:399
  72.2 11.7 %collective-permute-start.8 = (bf16[2,32,32,128]{3,2,1,0:T(8,128)(2,1)S(1)}, bf16[2,32,32,128]{3,2,1,0:T(8,128)(2,1)S(1)}, u32[]{:S(2)}, u32[]{:S(2)}) collective-permute-start(bf16[2,32,32,128]{3,2,1,0:T(8,128)(2,1)S(1)} %get-tuple-element.138), channel_id=1, source_target_pairs={{0,3},{1,0},{2,1},{3,2},{4,7},{5,4},{6,5},{7,6},{8,11},{9,8},{10,9... | collective-permute-start | bytes 1572872 | tf_op jit(solution)/shard_map/ppermute | solution.py:399
  83.8 7.7 %collective-permute-start.7 = (bf16[33,32,128]{2,1,0:T(8,128)(2,1)S(1)}, bf16[33,32,128]{2,1,0:T(8,128)(2,1)S(1)}, u32[]{:S(2)}, u32[]{:S(2)}) collective-permute-start(bf16[33,32,128]{2,1,0:T(8,128)(2,1)S(1)} %get-tuple-element.137.refs_7_), channel_id=1, source_target_pairs={{0,1},{1,2},{2,3},{3,0},{4,5},{5,6},{6,7},{7,4},{8,9},{9,10},{10,1... | collective-permute-start | bytes 811016 | tf_op jit(solution)/shard_map/ppermute | solution.py:399
  95.6 11.6 %collective-permute-start.12 = (bf16[2,32,32,128]{3,2,1,0:T(8,128)(2,1)S(1)}, bf16[2,32,32,128]{3,2,1,0:T(8,128)(2,1)S(1)}, u32[]{:S(2)}, u32[]{:S(2)}) collective-permute-start(bf16[2,32,32,128]{3,2,1,0:T(8,128)(2,1)S(1)} %get-tuple-element.149), channel_id=1, source_target_pairs={{0,3},{1,0},{2,1},{3,2},{4,7},{5,4},{6,5},{7,6},{8,11},{9,8},{10,9... | collective-permute-start | bytes 1572872 | tf_op jit(solution)/shard_map/ppermute | solution.py:399
  121.0 7.9 %collective-permute-start.13 = (bf16[33,32,128]{2,1,0:T(8,128)(2,1)S(1)}, bf16[33,32,128]{2,1,0:T(8,128)(2,1)S(1)}, u32[]{:S(2)}, u32[]{:S(2)}) collective-permute-start(bf16[33,32,128]{2,1,0:T(8,128)(2,1)S(1)} %get-tuple-element.153), channel_id=1, source_target_pairs={{0,1},{1,2},{2,3},{3,0},{4,5},{5,6},{6,7},{7,4},{8,9},{9,10},{10,1... | collective-permute-start | bytes 811016 | tf_op jit(solution)/shard_map/ppermute | solution.py:399
  121.3 13.8 %collective-permute-start.15 = (bf16[2,32,32,128]{3,2,1,0:T(8,128)(2,1)S(1)}, bf16[2,32,32,128]{3,2,1,0:T(8,128)(2,1)S(1)}, u32[]{:S(2)}, u32[]{:S(2)}) collective-permute-start(bf16[2,32,32,128]{3,2,1,0:T(8,128)(2,1)S(1)} %get-tuple-element.158), channel_id=1, source_target_pairs={{0,3},{1,0},{2,1},{3,2},{4,7},{5,4},{6,5},{7,6},{8,11},{9,8},{10,9... | collective-permute-start | bytes 1572872 | tf_op jit(solution)/shard_map/ppermute | solution.py:399
  160.6 9.3 %collective-permute-start.17 = (bf16[33,32,128]{2,1,0:T(8,128)(2,1)S(1)}, bf16[33,32,128]{2,1,0:T(8,128)(2,1)S(1)}, u32[]{:S(2)}, u32[]{:S(2)}) collective-permute-start(bf16[33,32,128]{2,1,0:T(8,128)(2,1)S(1)} %get-tuple-element.179.refs_8_), channel_id=1, source_target_pairs={{0,3},{1,0},{2,1},{3,2},{4,7},{5,4},{6,5},{7,6},{8,11},{9,8},{10,9... | collective-permute-start | bytes 811016 | tf_op jit(solution)/shard_map/ppermute | solution.py:399
  165.5 13.2 %collective-permute-start.19 = (bf16[2,32,32,128]{3,2,1,0:T(8,128)(2,1)S(1)}, bf16[2,32,32,128]{3,2,1,0:T(8,128)(2,1)S(1)}, u32[]{:S(2)}, u32[]{:S(2)}) collective-permute-start(bf16[2,32,32,128]{3,2,1,0:T(8,128)(2,1)S(1)} %get-tuple-element.192), channel_id=1, source_target_pairs={{0,1},{1,2},{2,3},{3,0},{4,5},{5,6},{6,7},{7,4},{8,9},{9,10},{10,1... | collective-permute-start | bytes 1572872 | tf_op jit(solution)/shard_map/ppermute | solution.py:399
  170.7 10.2 %collective-permute-start.18 = (bf16[33,32,128]{2,1,0:T(8,128)(2,1)S(1)}, bf16[33,32,128]{2,1,0:T(8,128)(2,1)S(1)}, u32[]{:S(2)}, u32[]{:S(2)}) collective-permute-start(bf16[33,32,128]{2,1,0:T(8,128)(2,1)S(1)} %get-tuple-element.191), channel_id=1, source_target_pairs={{0,3},{1,0},{2,1},{3,2},{4,7},{5,4},{6,5},{7,6},{8,11},{9,8},{10,9... | collective-permute-start | bytes 811016 | tf_op jit(solution)/shard_map/ppermute | solution.py:399
  176.8 10.9 %collective-permute-start.21 = (bf16[2,32,32,128]{3,2,1,0:T(8,128)(2,1)S(1)}, bf16[2,32,32,128]{3,2,1,0:T(8,128)(2,1)S(1)}, u32[]{:S(2)}, u32[]{:S(2)}) collective-permute-start(bf16[2,32,32,128]{3,2,1,0:T(8,128)(2,1)S(1)} %get-tuple-element.195), channel_id=1, source_target_pairs={{0,1},{1,2},{2,3},{3,0},{4,5},{5,6},{6,7},{7,4},{8,9},{9,10},{10,1... | collective-permute-start | bytes 1572872 | tf_op jit(solution)/shard_map/ppermute | solution.py:399
  197.9 10.4 %collective-permute-start.24 = (bf16[2,32,32,128]{3,2,1,0:T(8,128)(2,1)S(1)}, bf16[2,32,32,128]{3,2,1,0:T(8,128)(2,1)S(1)}, u32[]{:S(2)}, u32[]{:S(2)}) collective-permute-start(bf16[2,32,32,128]{3,2,1,0:T(8,128)(2,1)S(1)} %get-tuple-element.201), channel_id=1, source_target_pairs={{0,1},{1,2},{2,3},{3,0},{4,5},{5,6},{6,7},{7,4},{8,9},{9,10},{10,1... | collective-permute-start | bytes 1572872 | tf_op jit(solution)/shard_map/ppermute | solution.py:399
  208.1 11.3 %collective-permute-start.25 = (bf16[4,32,32,128]{3,2,1,0:T(8,128)(2,1)S(1)}, bf16[4,32,32,128]{3,2,1,0:T(8,128)(2,1)S(1)}, u32[]{:S(2)}, u32[]{:S(2)}) collective-permute-start(bf16[4,32,32,128]{3,2,1,0:T(8,128)(2,1)S(1)} %copy-done.6), channel_id=1, source_target_pairs={{0,4},{4,0},{8,12},{12,8},{16,20},{20,16},{24,28},{28,24},{32,36},... | collective-permute-start | bytes 3145736 | tf_op jit(solution)/shard_map/ppermute | solution.py:443
  219.1 10.9 %collective-permute-start.27 = (bf16[33,32,128]{2,1,0:T(8,128)(2,1)}, bf16[33,32,128]{2,1,0:T(8,128)(2,1)S(1)}, u32[]{:S(2)}, u32[]{:S(2)}) collective-permute-start(bf16[33,32,128]{2,1,0:T(8,128)(2,1)} %get-tuple-element.216), channel_id=1, source_target_pairs={{0,3},{1,0},{2,1},{3,2},{4,7},{5,4},{6,5},{7,6},{8,11},{9,8},{10,9... | collective-permute-start | bytes 811016 | tf_op jit(solution)/shard_map/ppermute | solution.py:399
  230.0 15.2 %collective-permute-start.29 = (bf16[2,32,32,128]{3,2,1,0:T(8,128)(2,1)S(1)}, bf16[2,32,32,128]{3,2,1,0:T(8,128)(2,1)S(1)}, u32[]{:S(2)}, u32[]{:S(2)}) collective-permute-start(bf16[2,32,32,128]{3,2,1,0:T(8,128)(2,1)S(1)} %get-tuple-element.220), channel_id=1, source_target_pairs={{0,1},{1,2},{2,3},{3,0},{4,5},{5,6},{6,7},{7,4},{8,9},{9,10},{10,1... | collective-permute-start | bytes 1572872 | tf_op jit(solution)/shard_map/ppermute | solution.py:399
  238.6 8.3 %collective-permute-start.28 = (bf16[33,32,128]{2,1,0:T(8,128)(2,1)S(1)}, bf16[33,32,128]{2,1,0:T(8,128)(2,1)S(1)}, u32[]{:S(2)}, u32[]{:S(2)}) collective-permute-start(bf16[33,32,128]{2,1,0:T(8,128)(2,1)S(1)} %get-tuple-element.219.refs_9_), channel_id=1, source_target_pairs={{0,3},{1,0},{2,1},{3,2},{4,7},{5,4},{6,5},{7,6},{8,11},{9,8},{10,9... | collective-permute-start | bytes 811016 | tf_op jit(solution)/shard_map/ppermute | solution.py:399
  250.3 14.1 %collective-permute-start.32 = (bf16[2,32,32,128]{3,2,1,0:T(8,128)(2,1)S(1)}, bf16[2,32,32,128]{3,2,1,0:T(8,128)(2,1)S(1)}, u32[]{:S(2)}, u32[]{:S(2)}) collective-permute-start(bf16[2,32,32,128]{3,2,1,0:T(8,128)(2,1)S(1)} %get-tuple-element.225), channel_id=1, source_target_pairs={{0,1},{1,2},{2,3},{3,0},{4,5},{5,6},{6,7},{7,4},{8,9},{9,10},{10,1... | collective-permute-start | bytes 1572872 | tf_op jit(solution)/shard_map/ppermute | solution.py:399
  260.8 11.0 %collective-permute-start.9 = (bf16[4,32,32,128]{3,2,1,0:T(8,128)(2,1)S(1)}, bf16[4,32,32,128]{3,2,1,0:T(8,128)(2,1)S(1)}, u32[]{:S(2)}, u32[]{:S(2)}) collective-permute-start(bf16[4,32,32,128]{3,2,1,0:T(8,128)(2,1)S(1)} %copy-done.5), channel_id=1, source_target_pairs={{0,4},{4,0},{8,12},{12,8},{16,20},{20,16},{24,28},{28,24},{32,36},... | collective-permute-start | bytes 3145736 | tf_op jit(solution)/shard_map/ppermute | solution.py:443
  (63 other events, 811.1 us)
Sparse Core Ops, SparseCore 0:
  230.1 106.3 reduce-scatter.1

commit v3 on v2

--- a/solution.py
+++ b/solution.py
@@ -16,7 +16,7 @@
 SM = pl.BlockSpec(memory_space=pltpu.SMEM)
 HBM = pl.BlockSpec(memory_space=pltpu.HBM)
 LIMIT = 10 * 2**20
-GRAD_LIMIT = 9 * 2**20
+GRAD_LIMIT = 10 * 2**20
 PARTS = 2
 
 
@@ -311,7 +311,7 @@
 def tile_grads(plan, turn, info, normed_parts, error_parts, share, parts):
     G, T, B, M = plan.grid, plan.rows, plan.tile, plan.units
     local = plan.slots // parts
-    steps = 8
+    steps = 4
     chunk = local // steps
     tokens = M * T
 
@@ -322,13 +322,16 @@
 
         @pl.when(step == 0)
         def _():
-            for b in range(G):
+            def arrange(b, carry):
                 for p in range(parts):
                     for m in range(M):
                         at = p * tokens + m * T
                         flat[b, at:at + T, :] = errors[p][m, b]
                     whole = jnp.concatenate([normeds[p][m, b] for m in range(M)], axis=0)
                     turned[b, :, p * tokens:(p + 1) * tokens] = whole.T
+                return carry
+
+            each_block(G, arrange)
 
         half = tab[plan.half]
         live = tab[turn]

time: 362 us -> 368 us (1.017); the launches traced: 356 us -> 368 us
  starting transfers between devices: 46.9 us -> 72.5 us
  Pallas kernels: 93.6 us -> 85 us
  waiting for transfers between devices: 118 us -> 113 us
    ppermute x30, starting transfers between devices: 46.6 us -> 72.3 us  [ring(): lax.ppermute(part, 'section', [(i, (i + by) % sections) for i in range(se...]
    pallas_call x22, Pallas kernels: 79.1 us -> 72.7 us  [tick_call(): pl.pallas_call(kernel, in_specs=[SM] + [VM] * (len(names) - 1 + len(pack)...]
  transfers between devices with their start and end apart: 35 -> 35, of which waited for: 26 -> 24; matrix products, arithmetic and copies ran while one was open for 0% -> 0% of each run, Pallas kernels for 17% -> 15%
where the time goes in v3:
time: 368 us
  waiting for transfers between devices  113 us (31%)
  Pallas kernels  85 us (23%)
  starting transfers between devices  72.5 us (20%)
  blocking collectives  63.1 us (17%)
  local copies, waits for them, and re-layouts  18.3 us (5%)
  between operations  14.1 us (4%)
    ppermute x30, waiting for transfers between devices, ring(): lax.ppermute(part, 'section', [(i, (i + by) % sections) for i in range(se...  110 us
    pallas_call x22, Pallas kernels, tick_call(): pl.pallas_call(kernel, in_specs=[SM] + [VM] * (len(names) - 1 + len(pack)...  72.7 us
    ppermute x30, starting transfers between devices, ring(): lax.ppermute(part, 'section', [(i, (i + by) % sections) for i in range(se...  72.3 us
    all_to_all x1, blocking collectives, trade(): lax.all_to_all(part.reshape(members, share, tile, tile), 'dp', 0, 0, axis...  63.1 us
    unnamed x104, local copies, waits for them, and re-layouts  17.5 us
    pallas_call x2, Pallas kernels, tile_grads(): pl.pallas_call(kernel, grid_spec=pltpu.PrefetchScalarGridSpec(num_scalar_...  11.3 us
  transfers between devices with their start and end apart: 35, of which 24 were waited for; matrix products, arithmetic and copies ran while one was open for 0% of the time, Pallas kernels for 15%

profile of v3, /device:TPU:0, one launch (start us, length us, event | category | flops | bytes accessed | tf_op | source)
XLA Modules:
  0.0 367.5 jit_solution(15236109195876958526)
XLA Ops:
  7.3 5.8 %copy-done = bf16[2,1,256,128,128]{4,3,2,1,0:T(8,128)(2,1)S(1)} copy-done((bf16[2,1,256,128,128]{4,3,2,1,0:T(8,128)(2,1)S(1)}, bf16[2,1,256,128,128]{4,3,2,1,0:T(8,128)(2,1)}, u32[]{:S(2)}) %copy-start) | copy-done | bytes 16777240
  18.2 5.0 %collective-permute-start = (bf16[33,32,128]{2,1,0:T(8,128)(2,1)S(1)}, bf16[33,32,128]{2,1,0:T(8,128)(2,1)S(1)}, u32[]{:S(2)}, u32[]{:S(2)}) collective-permute-start(bf16[33,32,128]{2,1,0:T(8,128)(2,1)S(1)} %get-tuple-element.117), channel_id=1, source_target_pairs={{0,1},{1,2},{2,3},{3,0},{4,5},{5,6},{6,7},{7,4},{8,9},{9,10},{10,1... | collective-permute-start | bytes 811016 | tf_op jit(solution)/shard_map/ppermute | solution.py:402
  23.2 7.7 %collective-permute-done.refs_4_ = bf16[33,32,128]{2,1,0:T(8,128)(2,1)S(1)} collective-permute-done((bf16[33,32,128]{2,1,0:T(8,128)(2,1)S(1)}, bf16[33,32,128]{2,1,0:T(8,128)(2,1)S(1)}, u32[]{:S(2)}, u32[]{:S(2)}) %collective-permute-start) | collective-permute-done | bytes 270368 | tf_op jit(solution)/shard_map/ppermute | solution.py:402
  39.0 5.5 %collective-permute-done.1.refs_4_ = bf16[33,32,128]{2,1,0:T(8,128)(2,1)S(1)} collective-permute-done((bf16[33,32,128]{2,1,0:T(8,128)(2,1)S(1)}, bf16[33,32,128]{2,1,0:T(8,128)(2,1)S(1)}, u32[]{:S(2)}, u32[]{:S(2)}) %collective-permute-start.1) | collective-permute-done | bytes 270368 | tf_op jit(solution)/shard_map/ppermute | solution.py:402
  52.1 4.6 %collective-permute-done.2.refs_4_ = bf16[33,32,128]{2,1,0:T(8,128)(2,1)S(1)} collective-permute-done((bf16[33,32,128]{2,1,0:T(8,128)(2,1)S(1)}, bf16[33,32,128]{2,1,0:T(8,128)(2,1)S(1)}, u32[]{:S(2)}, u32[]{:S(2)}) %collective-permute-start.2) | collective-permute-done | bytes 270368 | tf_op jit(solution)/shard_map/ppermute | solution.py:402
  61.5 6.2 %collective-permute-done.4.refs_5_ = bf16[33,32,128]{2,1,0:T(8,128)(2,1)S(1)} collective-permute-done((bf16[33,32,128]{2,1,0:T(8,128)(2,1)S(1)}, bf16[33,32,128]{2,1,0:T(8,128)(2,1)S(1)}, u32[]{:S(2)}, u32[]{:S(2)}) %collective-permute-start.4) | collective-permute-done | bytes 270368 | tf_op jit(solution)/shard_map/ppermute | solution.py:402
  83.5 7.6 %collective-permute-done.7.refs_5_ = bf16[33,32,128]{2,1,0:T(8,128)(2,1)S(1)} collective-permute-done((bf16[33,32,128]{2,1,0:T(8,128)(2,1)S(1)}, bf16[33,32,128]{2,1,0:T(8,128)(2,1)S(1)}, u32[]{:S(2)}, u32[]{:S(2)}) %collective-permute-start.7) | collective-permute-done | bytes 270368 | tf_op jit(solution)/shard_map/ppermute | solution.py:402
  106.8 7.6 %collective-permute-done.11.refs_4_ = bf16[33,32,128]{2,1,0:T(8,128)(2,1)S(1)} collective-permute-done((bf16[33,32,128]{2,1,0:T(8,128)(2,1)S(1)}, bf16[33,32,128]{2,1,0:T(8,128)(2,1)S(1)}, u32[]{:S(2)}, u32[]{:S(2)}) %collective-permute-start.11) | collective-permute-done | bytes 270368 | tf_op jit(solution)/shard_map/ppermute | solution.py:402
  114.5 6.2 %forward_tick.19 = (bf16[33,32,128]{2,1,0:T(8,128)(2,1)S(1)}, bf16[32,32,128]{2,1,0:T(8,128)(2,1)}, bf16[32,32,128]{2,1,0:T(8,128)(2,1)}, f32[32,128]{1,0:T(8,12...) custom-call(s32[1028]{0:T(1024)S(1)} %concatenate.3.refs_0_.tab, ...), custom_call_target="tpu_custom_call", output_to_operand_aliasing={{4}: (7, {}), {5}: (8, {}), {6}: (9, {})} | custom-call | tf_op jit(solution)/shard_map/forward_tick/pallas_call | solution.py:298
  128.6 6.1 %forward_tick.20 = (bf16[33,32,128]{2,1,0:T(8,128)(2,1)S(1)}, bf16[32,32,128]{2,1,0:T(8,128)(2,1)}, bf16[32,32,128]{2,1,0:T(8,128)(2,1)}, f32[32,128]{1,0:T(8,12...) custom-call(s32[1028]{0:T(1024)S(1)} %concatenate.3.refs_0_.tab, ...), custom_call_target="tpu_custom_call", output_to_operand_aliasing={{4}: (6, {}), {5}: (7, {}), {6}: (8, {})} | custom-call | tf_op jit(solution)/shard_map/forward_tick/pallas_call | solution.py:298
  134.7 7.6 %collective-permute-done.14.refs_4_ = bf16[33,32,128]{2,1,0:T(8,128)(2,1)S(1)} collective-permute-done((bf16[33,32,128]{2,1,0:T(8,128)(2,1)S(1)}, bf16[33,32,128]{2,1,0:T(8,128)(2,1)S(1)}, u32[]{:S(2)}, u32[]{:S(2)}) %collective-permute-start.14) | collective-permute-done | bytes 270368 | tf_op jit(solution)/shard_map/ppermute | solution.py:402
  142.4 6.4 %forward_tick.21 = (bf16[33,32,128]{2,1,0:T(8,128)(2,1)}, bf16[32,32,128]{2,1,0:T(8,128)(2,1)S(1)}, bf16[32,32,128]{2,1,0:T(8,128)(2,1)S(1)}, f32[32,128]{1,0:T(...) custom-call(s32[1028]{0:T(1024)S(1)} %concatenate.3.refs_0_.tab, ...), custom_call_target="tpu_custom_call", output_to_operand_aliasing={{4}: (6, {}), {5}: (7, {}), {6}: (8, {})} | custom-call | tf_op jit(solution)/shard_map/forward_tick/pallas_call | solution.py:298
  155.7 6.6 %collective-permute-done.16.refs_7_ = bf16[33,32,128]{2,1,0:T(8,128)(2,1)S(1)} collective-permute-done((bf16[33,32,128]{2,1,0:T(8,128)(2,1)S(1)}, bf16[33,32,128]{2,1,0:T(8,128)(2,1)S(1)}, u32[]{:S(2)}, u32[]{:S(2)}) %collective-permute-start.16) | collective-permute-done | bytes 270368 | tf_op jit(solution)/shard_map/ppermute | solution.py:402
  163.0 7.7 %collective-permute-start.17 = (bf16[33,32,128]{2,1,0:T(8,128)(2,1)S(1)}, bf16[33,32,128]{2,1,0:T(8,128)(2,1)S(1)}, u32[]{:S(2)}, u32[]{:S(2)}) collective-permute-start(bf16[33,32,128]{2,1,0:T(8,128)(2,1)S(1)} %get-tuple-element.179.refs_8_), channel_id=1, source_target_pairs={{0,3},{1,0},{2,1},{3,2},{4,7},{5,4},{6,5},{7,6},{8,11},{9,8},{10,9... | collective-permute-start | bytes 811016 | tf_op jit(solution)/shard_map/ppermute | solution.py:402
  170.7 5.8 %collective-permute-done.17.refs_7_ = bf16[33,32,128]{2,1,0:T(8,128)(2,1)S(1)} collective-permute-done((bf16[33,32,128]{2,1,0:T(8,128)(2,1)S(1)}, bf16[33,32,128]{2,1,0:T(8,128)(2,1)S(1)}, u32[]{:S(2)}, u32[]{:S(2)}) %collective-permute-start.17) | collective-permute-done | bytes 270368 | tf_op jit(solution)/shard_map/ppermute | solution.py:402
  177.4 7.7 %collective-permute-start.18 = (bf16[33,32,128]{2,1,0:T(8,128)(2,1)S(1)}, bf16[33,32,128]{2,1,0:T(8,128)(2,1)S(1)}, u32[]{:S(2)}, u32[]{:S(2)}) collective-permute-start(bf16[33,32,128]{2,1,0:T(8,128)(2,1)S(1)} %get-tuple-element.191), channel_id=1, source_target_pairs={{0,3},{1,0},{2,1},{3,2},{4,7},{5,4},{6,5},{7,6},{8,11},{9,8},{10,9... | collective-permute-start | bytes 811016 | tf_op jit(solution)/shard_map/ppermute | solution.py:402
  193.5 4.9 %collective-permute-start.20 = (bf16[33,32,128]{2,1,0:T(8,128)(2,1)S(1)}, bf16[33,32,128]{2,1,0:T(8,128)(2,1)S(1)}, u32[]{:S(2)}, u32[]{:S(2)}) collective-permute-start(bf16[33,32,128]{2,1,0:T(8,128)(2,1)S(1)} %get-tuple-element.194.refs_11_), channel_id=1, source_target_pairs={{0,3},{1,0},{2,1},{3,2},{4,7},{5,4},{6,5},{7,6},{8,11},{9,8},{10,9... | collective-permute-start | bytes 811016 | tf_op jit(solution)/shard_map/ppermute | solution.py:402
  231.2 4.8 %collective-permute-start.27 = (bf16[33,32,128]{2,1,0:T(8,128)(2,1)}, bf16[33,32,128]{2,1,0:T(8,128)(2,1)S(1)}, u32[]{:S(2)}, u32[]{:S(2)}) collective-permute-start(bf16[33,32,128]{2,1,0:T(8,128)(2,1)} %get-tuple-element.216), channel_id=1, source_target_pairs={{0,3},{1,0},{2,1},{3,2},{4,7},{5,4},{6,5},{7,6},{8,11},{9,8},{10,9... | collective-permute-start | bytes 811016 | tf_op jit(solution)/shard_map/ppermute | solution.py:402
  237.2 5.6 %tile_grads.2 = bf16[128,128,128]{2,1,0:T(8,128)(2,1)} custom-call(s32[1028]{0:T(1024)S(1)} %concatenate.3.refs_0_.tab, bf16[4,32,32,128]{3,2,1,0:T(8,128)(2,1)S(1)} %copy-done.6, bf16[4,32,32,128]{3,2,1,0:T(8,128)(2,1)S(1)} %collective-permute-done.25.refs_1_, bf16[4,32,32,128]{3,2,1,0:T(8,128)(2,1)S(1)} %copy-done.7, ...), custom_call_target="tpu_custom_call" | custom-call | flops 1073741824 | bytes 25165824 | tf_op jit(solution)/shard_map/tile_grads/pallas_call | solution.py:346
  248.7 5.2 %collective-permute-start.28 = (bf16[33,32,128]{2,1,0:T(8,128)(2,1)S(1)}, bf16[33,32,128]{2,1,0:T(8,128)(2,1)S(1)}, u32[]{:S(2)}, u32[]{:S(2)}) collective-permute-start(bf16[33,32,128]{2,1,0:T(8,128)(2,1)S(1)} %get-tuple-element.219.refs_9_), channel_id=1, source_target_pairs={{0,3},{1,0},{2,1},{3,2},{4,7},{5,4},{6,5},{7,6},{8,11},{9,8},{10,9... | collective-permute-start | bytes 811016 | tf_op jit(solution)/shard_map/ppermute | solution.py:402
  265.7 5.3 %collective-permute-done.30.refs_7_ = bf16[33,32,128]{2,1,0:T(8,128)(2,1)S(1)} collective-permute-done((bf16[33,32,128]{2,1,0:T(8,128)(2,1)S(1)}, bf16[33,32,128]{2,1,0:T(8,128)(2,1)S(1)}, u32[]{:S(2)}, u32[]{:S(2)}) %collective-permute-start.30) | collective-permute-done | bytes 270368 | tf_op jit(solution)/shard_map/ppermute | solution.py:402
  273.9 5.1 %collective-permute-done.32.refs_8_ = bf16[2,32,32,128]{3,2,1,0:T(8,128)(2,1)S(1)} collective-permute-done((bf16[2,32,32,128]{3,2,1,0:T(8,128)(2,1)S(1)}, bf16[2,32,32,128]{3,2,1,0:T(8,128)(2,1)S(1)}, u32[]{:S(2)}, u32[]{:S(2)}) %collective-permute-start.32) | collective-permute-done | bytes 524320 | tf_op jit(solution)/shard_map/ppermute | solution.py:402
  289.0 5.7 %tile_grads.3 = bf16[128,128,128]{2,1,0:T(8,128)(2,1)} custom-call(s32[1028]{0:T(1024)S(1)} %concatenate.3.refs_0_.tab, bf16[4,32,32,128]{3,2,1,0:T(8,128)(2,1)S(1)} %copy-done.5, bf16[4,32,32,128]{3,2,1,0:T(8,128)(2,1)S(1)} %collective-permute-done.9.refs_1_, bf16[4,32,32,128]{3,2,1,0:T(8,128)(2,1)S(1)} %copy-done.8, ...), custom_call_target="tpu_custom_call" | custom-call | flops 1073741824 | bytes 25165824 | tf_op jit(solution)/shard_map/tile_grads/pallas_call | solution.py:346
  294.7 63.1 %all_to_all.5.given = bf16[16,8,128,128]{3,2,1,0:T(8,128)(2,1)S(1)} all-to-all(bf16[16,8,128,128]{3,2,1,0:T(8,128)(2,1)} %bitcast.68), channel_id=1, replica_groups={{0,8,16,24,32,40,48,56,64,72,80,88,96,104,112,120},{4,12,20,28,36,44,52..., dimensions={0} | all-to-all | bytes 8388608 | tf_op jit(solution)/shard_map/all_to_all | solution.py:453
  (181 shorter events, 149.4 us)
Async XLA Ops:
  6.5 352.3 %reduce-scatter.2.cloned.1.call-start = ((), (), s32[]{:S(2)}) async-start(), calls=%async_computation.2 | async-start | bytes 4456448 | tf_op jit(solution)/shard_map/reduce_scatter | solution.py:462
  18.2 12.7 %collective-permute-start = (bf16[33,32,128]{2,1,0:T(8,128)(2,1)S(1)}, bf16[33,32,128]{2,1,0:T(8,128)(2,1)S(1)}, u32[]{:S(2)}, u32[]{:S(2)}) collective-permute-start(bf16[33,32,128]{2,1,0:T(8,128)(2,1)S(1)} %get-tuple-element.117), channel_id=1, source_target_pairs={{0,1},{1,2},{2,3},{3,0},{4,5},{5,6},{6,7},{7,4},{8,9},{9,10},{10,1... | collective-permute-start | bytes 811016 | tf_op jit(solution)/shard_map/ppermute | solution.py:402
  33.8 10.7 %collective-permute-start.1 = (bf16[33,32,128]{2,1,0:T(8,128)(2,1)S(1)}, bf16[33,32,128]{2,1,0:T(8,128)(2,1)S(1)}, u32[]{:S(2)}, u32[]{:S(2)}) collective-permute-start(bf16[33,32,128]{2,1,0:T(8,128)(2,1)S(1)} %get-tuple-element.121.refs_5_), channel_id=1, source_target_pairs={{0,1},{1,2},{2,3},{3,0},{4,5},{5,6},{6,7},{7,4},{8,9},{9,10},{10,1... | collective-permute-start | bytes 811016 | tf_op jit(solution)/shard_map/ppermute | solution.py:402
  35.8 16.3 %collective-permute-start.3 = (bf16[2,32,32,128]{3,2,1,0:T(8,128)(2,1)S(1)}, bf16[2,32,32,128]{3,2,1,0:T(8,128)(2,1)S(1)}, u32[]{:S(2)}, u32[]{:S(2)}) collective-permute-start(bf16[2,32,32,128]{3,2,1,0:T(8,128)(2,1)S(1)} %get-tuple-element.129), channel_id=1, source_target_pairs={{0,3},{1,0},{2,1},{3,2},{4,7},{5,4},{6,5},{7,6},{8,11},{9,8},{10,9... | collective-permute-start | bytes 1572872 | tf_op jit(solution)/shard_map/ppermute | solution.py:402
  47.3 9.4 %collective-permute-start.2 = (bf16[33,32,128]{2,1,0:T(8,128)(2,1)S(1)}, bf16[33,32,128]{2,1,0:T(8,128)(2,1)S(1)}, u32[]{:S(2)}, u32[]{:S(2)}) collective-permute-start(bf16[33,32,128]{2,1,0:T(8,128)(2,1)S(1)} %get-tuple-element.128), channel_id=1, source_target_pairs={{0,1},{1,2},{2,3},{3,0},{4,5},{5,6},{6,7},{7,4},{8,9},{9,10},{10,1... | collective-permute-start | bytes 811016 | tf_op jit(solution)/shard_map/ppermute | solution.py:402
  48.4 13.1 %collective-permute-start.5 = (bf16[2,32,32,128]{3,2,1,0:T(8,128)(2,1)S(1)}, bf16[2,32,32,128]{3,2,1,0:T(8,128)(2,1)S(1)}, u32[]{:S(2)}, u32[]{:S(2)}) collective-permute-start(bf16[2,32,32,128]{3,2,1,0:T(8,128)(2,1)S(1)} %get-tuple-element.132), channel_id=1, source_target_pairs={{0,3},{1,0},{2,1},{3,2},{4,7},{5,4},{6,5},{7,6},{8,11},{9,8},{10,9... | collective-permute-start | bytes 1572872 | tf_op jit(solution)/shard_map/ppermute | solution.py:402
  71.8 11.7 %collective-permute-start.8 = (bf16[2,32,32,128]{3,2,1,0:T(8,128)(2,1)S(1)}, bf16[2,32,32,128]{3,2,1,0:T(8,128)(2,1)S(1)}, u32[]{:S(2)}, u32[]{:S(2)}) collective-permute-start(bf16[2,32,32,128]{3,2,1,0:T(8,128)(2,1)S(1)} %get-tuple-element.138), channel_id=1, source_target_pairs={{0,3},{1,0},{2,1},{3,2},{4,7},{5,4},{6,5},{7,6},{8,11},{9,8},{10,9... | collective-permute-start | bytes 1572872 | tf_op jit(solution)/shard_map/ppermute | solution.py:402
  95.2 11.6 %collective-permute-start.12 = (bf16[2,32,32,128]{3,2,1,0:T(8,128)(2,1)S(1)}, bf16[2,32,32,128]{3,2,1,0:T(8,128)(2,1)S(1)}, u32[]{:S(2)}, u32[]{:S(2)}) collective-permute-start(bf16[2,32,32,128]{3,2,1,0:T(8,128)(2,1)S(1)} %get-tuple-element.149), channel_id=1, source_target_pairs={{0,3},{1,0},{2,1},{3,2},{4,7},{5,4},{6,5},{7,6},{8,11},{9,8},{10,9... | collective-permute-start | bytes 1572872 | tf_op jit(solution)/shard_map/ppermute | solution.py:402
  120.9 13.8 %collective-permute-start.15 = (bf16[2,32,32,128]{3,2,1,0:T(8,128)(2,1)S(1)}, bf16[2,32,32,128]{3,2,1,0:T(8,128)(2,1)S(1)}, u32[]{:S(2)}, u32[]{:S(2)}) collective-permute-start(bf16[2,32,32,128]{3,2,1,0:T(8,128)(2,1)S(1)} %get-tuple-element.158), channel_id=1, source_target_pairs={{0,3},{1,0},{2,1},{3,2},{4,7},{5,4},{6,5},{7,6},{8,11},{9,8},{10,9... | collective-permute-start | bytes 1572872 | tf_op jit(solution)/shard_map/ppermute | solution.py:402
  153.0 9.3 %collective-permute-start.16 = (bf16[33,32,128]{2,1,0:T(8,128)(2,1)S(1)}, bf16[33,32,128]{2,1,0:T(8,128)(2,1)S(1)}, u32[]{:S(2)}, u32[]{:S(2)}) collective-permute-start(bf16[33,32,128]{2,1,0:T(8,128)(2,1)S(1)} %get-tuple-element.177), channel_id=1, source_target_pairs={{0,3},{1,0},{2,1},{3,2},{4,7},{5,4},{6,5},{7,6},{8,11},{9,8},{10,9... | collective-permute-start | bytes 811016 | tf_op jit(solution)/shard_map/ppermute | solution.py:402
  163.0 13.5 %collective-permute-start.17 = (bf16[33,32,128]{2,1,0:T(8,128)(2,1)S(1)}, bf16[33,32,128]{2,1,0:T(8,128)(2,1)S(1)}, u32[]{:S(2)}, u32[]{:S(2)}) collective-permute-start(bf16[33,32,128]{2,1,0:T(8,128)(2,1)S(1)} %get-tuple-element.179.refs_8_), channel_id=1, source_target_pairs={{0,3},{1,0},{2,1},{3,2},{4,7},{5,4},{6,5},{7,6},{8,11},{9,8},{10,9... | collective-permute-start | bytes 811016 | tf_op jit(solution)/shard_map/ppermute | solution.py:402
  170.7 14.7 %collective-permute-start.19 = (bf16[2,32,32,128]{3,2,1,0:T(8,128)(2,1)S(1)}, bf16[2,32,32,128]{3,2,1,0:T(8,128)(2,1)S(1)}, u32[]{:S(2)}, u32[]{:S(2)}) collective-permute-start(bf16[2,32,32,128]{3,2,1,0:T(8,128)(2,1)S(1)} %get-tuple-element.192), channel_id=1, source_target_pairs={{0,1},{1,2},{2,3},{3,0},{4,5},{5,6},{6,7},{7,4},{8,9},{9,10},{10,1... | collective-permute-start | bytes 1572872 | tf_op jit(solution)/shard_map/ppermute | solution.py:402
  177.4 12.6 %collective-permute-start.18 = (bf16[33,32,128]{2,1,0:T(8,128)(2,1)S(1)}, bf16[33,32,128]{2,1,0:T(8,128)(2,1)S(1)}, u32[]{:S(2)}, u32[]{:S(2)}) collective-permute-start(bf16[33,32,128]{2,1,0:T(8,128)(2,1)S(1)} %get-tuple-element.191), channel_id=1, source_target_pairs={{0,3},{1,0},{2,1},{3,2},{4,7},{5,4},{6,5},{7,6},{8,11},{9,8},{10,9... | collective-permute-start | bytes 811016 | tf_op jit(solution)/shard_map/ppermute | solution.py:402
  185.0 13.4 %collective-permute-start.21 = (bf16[2,32,32,128]{3,2,1,0:T(8,128)(2,1)S(1)}, bf16[2,32,32,128]{3,2,1,0:T(8,128)(2,1)S(1)}, u32[]{:S(2)}, u32[]{:S(2)}) collective-permute-start(bf16[2,32,32,128]{3,2,1,0:T(8,128)(2,1)S(1)} %get-tuple-element.195), channel_id=1, source_target_pairs={{0,1},{1,2},{2,3},{3,0},{4,5},{5,6},{6,7},{7,4},{8,9},{9,10},{10,1... | collective-permute-start | bytes 1572872 | tf_op jit(solution)/shard_map/ppermute | solution.py:402
  193.5 8.9 %collective-permute-start.20 = (bf16[33,32,128]{2,1,0:T(8,128)(2,1)S(1)}, bf16[33,32,128]{2,1,0:T(8,128)(2,1)S(1)}, u32[]{:S(2)}, u32[]{:S(2)}) collective-permute-start(bf16[33,32,128]{2,1,0:T(8,128)(2,1)S(1)} %get-tuple-element.194.refs_11_), channel_id=1, source_target_pairs={{0,3},{1,0},{2,1},{3,2},{4,7},{5,4},{6,5},{7,6},{8,11},{9,8},{10,9... | collective-permute-start | bytes 811016 | tf_op jit(solution)/shard_map/ppermute | solution.py:402
  206.1 8.5 %collective-permute-start.22 = (bf16[33,32,128]{2,1,0:T(8,128)(2,1)S(1)}, bf16[33,32,128]{2,1,0:T(8,128)(2,1)S(1)}, u32[]{:S(2)}, u32[]{:S(2)}) collective-permute-start(bf16[33,32,128]{2,1,0:T(8,128)(2,1)S(1)} %get-tuple-element.197), channel_id=1, source_target_pairs={{0,3},{1,0},{2,1},{3,2},{4,7},{5,4},{6,5},{7,6},{8,11},{9,8},{10,9... | collective-permute-start | bytes 811016 | tf_op jit(solution)/shard_map/ppermute | solution.py:402
  210.6 12.1 %collective-permute-start.24 = (bf16[2,32,32,128]{3,2,1,0:T(8,128)(2,1)S(1)}, bf16[2,32,32,128]{3,2,1,0:T(8,128)(2,1)S(1)}, u32[]{:S(2)}, u32[]{:S(2)}) collective-permute-start(bf16[2,32,32,128]{3,2,1,0:T(8,128)(2,1)S(1)} %get-tuple-element.201), channel_id=1, source_target_pairs={{0,1},{1,2},{2,3},{3,0},{4,5},{5,6},{6,7},{7,4},{8,9},{9,10},{10,1... | collective-permute-start | bytes 1572872 | tf_op jit(solution)/shard_map/ppermute | solution.py:402
  222.8 13.2 %collective-permute-start.25 = (bf16[4,32,32,128]{3,2,1,0:T(8,128)(2,1)S(1)}, bf16[4,32,32,128]{3,2,1,0:T(8,128)(2,1)S(1)}, u32[]{:S(2)}, u32[]{:S(2)}) collective-permute-start(bf16[4,32,32,128]{3,2,1,0:T(8,128)(2,1)S(1)} %copy-done.6), channel_id=1, source_target_pairs={{0,4},{4,0},{8,12},{12,8},{16,20},{20,16},{24,28},{28,24},{32,36},... | collective-permute-start | bytes 3145736 | tf_op jit(solution)/shard_map/ppermute | solution.py:446
  231.2 11.6 %collective-permute-start.27 = (bf16[33,32,128]{2,1,0:T(8,128)(2,1)}, bf16[33,32,128]{2,1,0:T(8,128)(2,1)S(1)}, u32[]{:S(2)}, u32[]{:S(2)}) collective-permute-start(bf16[33,32,128]{2,1,0:T(8,128)(2,1)} %get-tuple-element.216), channel_id=1, source_target_pairs={{0,3},{1,0},{2,1},{3,2},{4,7},{5,4},{6,5},{7,6},{8,11},{9,8},{10,9... | collective-permute-start | bytes 811016 | tf_op jit(solution)/shard_map/ppermute | solution.py:402
  242.8 15.0 %collective-permute-start.29 = (bf16[2,32,32,128]{3,2,1,0:T(8,128)(2,1)S(1)}, bf16[2,32,32,128]{3,2,1,0:T(8,128)(2,1)S(1)}, u32[]{:S(2)}, u32[]{:S(2)}) collective-permute-start(bf16[2,32,32,128]{3,2,1,0:T(8,128)(2,1)S(1)} %get-tuple-element.220), channel_id=1, source_target_pairs={{0,1},{1,2},{2,3},{3,0},{4,5},{5,6},{6,7},{7,4},{8,9},{9,10},{10,1... | collective-permute-start | bytes 1572872 | tf_op jit(solution)/shard_map/ppermute | solution.py:402
  248.7 10.8 %collective-permute-start.28 = (bf16[33,32,128]{2,1,0:T(8,128)(2,1)S(1)}, bf16[33,32,128]{2,1,0:T(8,128)(2,1)S(1)}, u32[]{:S(2)}, u32[]{:S(2)}) collective-permute-start(bf16[33,32,128]{2,1,0:T(8,128)(2,1)S(1)} %get-tuple-element.219.refs_9_), channel_id=1, source_target_pairs={{0,3},{1,0},{2,1},{3,2},{4,7},{5,4},{6,5},{7,6},{8,11},{9,8},{10,9... | collective-permute-start | bytes 811016 | tf_op jit(solution)/shard_map/ppermute | solution.py:402
  261.9 9.1 %collective-permute-start.30 = (bf16[33,32,128]{2,1,0:T(8,128)(2,1)S(1)}, bf16[33,32,128]{2,1,0:T(8,128)(2,1)S(1)}, u32[]{:S(2)}, u32[]{:S(2)}) collective-permute-start(bf16[33,32,128]{2,1,0:T(8,128)(2,1)S(1)} %get-tuple-element.222), channel_id=1, source_target_pairs={{0,3},{1,0},{2,1},{3,2},{4,7},{5,4},{6,5},{7,6},{8,11},{9,8},{10,9... | collective-permute-start | bytes 811016 | tf_op jit(solution)/shard_map/ppermute | solution.py:402
  264.1 14.9 %collective-permute-start.32 = (bf16[2,32,32,128]{3,2,1,0:T(8,128)(2,1)S(1)}, bf16[2,32,32,128]{3,2,1,0:T(8,128)(2,1)S(1)}, u32[]{:S(2)}, u32[]{:S(2)}) collective-permute-start(bf16[2,32,32,128]{3,2,1,0:T(8,128)(2,1)S(1)} %get-tuple-element.225), channel_id=1, source_target_pairs={{0,1},{1,2},{2,3},{3,0},{4,5},{5,6},{6,7},{7,4},{8,9},{9,10},{10,1... | collective-permute-start | bytes 1572872 | tf_op jit(solution)/shard_map/ppermute | solution.py:402
  273.9 11.0 %collective-permute-start.9 = (bf16[4,32,32,128]{3,2,1,0:T(8,128)(2,1)S(1)}, bf16[4,32,32,128]{3,2,1,0:T(8,128)(2,1)S(1)}, u32[]{:S(2)}, u32[]{:S(2)}) collective-permute-start(bf16[4,32,32,128]{3,2,1,0:T(8,128)(2,1)S(1)} %copy-done.5), channel_id=1, source_target_pairs={{0,4},{4,0},{8,12},{12,8},{16,20},{20,16},{24,28},{28,24},{32,36},... | collective-permute-start | bytes 3145736 | tf_op jit(solution)/shard_map/ppermute | solution.py:446
  (63 other events, 902.6 us)
Sparse Core Ops, SparseCore 0:
  243.0 105.5 reduce-scatter.1
